TPU v7x, 128 devices: a whole 4x4x4 slice. The times are simulated.
128 devices in a mesh: frame: 4 (over z), panel: 32 (over x, y, core).
Axes of the slice: x: 4, y: 4, z: 4, core: 2. Of those that a mesh axis runs over, the one named last changes fastest.
Arguments:
- spline_index: int32 [16384, 2, 4, 256], P(('frame', 'panel')), may hold values from 0 to 124
- spline_frac: bfloat16 [16384, 2, 4, 256], P(('frame', 'panel')), may hold values from 0 to 1
- projection: bfloat16 [16384, 2, 4, 256], P(('frame', 'panel')), may hold values from -6 to 6
- forces: bfloat16 [16384, 256], P(('frame', 'panel')), may hold values from -6 to 6
- row_owner: int32 [16384, 1], P(('frame', 'panel')), may hold values from 0 to 127, as said below
- row_offset: int32 [16384], P(('frame', 'panel')), may hold values from 0 to 21
Outputs:
- normal_band: float32 [2816, 2, 128, 128], P(('frame', 'panel'))
- normal_rhs: float32 [2816, 128], P(('frame', 'panel'))
Inputs may be any that keep to these rules, and one draw needn't show every extreme that they name: `row_owner`: among the row tiles of one device, no owner index is named by more than 2 tiles, and some owner index is named by exactly 2. Every owner index is named by some row tile.
All inputs are finite; a program needn't handle non-finite values.
Results may differ from a plain program's by a relative error of at most 0.0029.
Values may be sent and summed in bfloat16 or wider, within the bound.
No kernel may reach another device: no remote copies, remote signals or barrier semaphores. Data moves between devices by JAX's collectives and lax.ppermute only.
A program may use at most 64 MiB of HBM per device.

v0:
```python
import jax
import jax.numpy as jnp
from jax import lax
from jax.sharding import PartitionSpec as P

CO = 128
BLK_DEV = 22


def shifted(block, axis, distance):
    devices = range(lax.axis_size(axis))
    route = [((i - distance) % len(devices), i) for i in devices]
    return lax.ppermute(block, axis, route)


def basis_tiles(spline_index, spline_frac, projection, column_count):
    columns = lax.broadcasted_iota(jnp.int32, (1, 1, 1, column_count), 3)
    summed = jnp.zeros(spline_index.shape[:2] + (spline_index.shape[3], column_count), jnp.float32)
    for neighbor in range(spline_index.shape[2]):
        offset = columns - spline_index[:, :, neighbor, :, None]
        position = spline_frac[:, :, neighbor, :, None].astype(jnp.float32)
        weight = projection[:, :, neighbor, :, None].astype(jnp.float32)
        one_minus = 1.0 - position
        pos_square = position * position
        pos_cube = pos_square * position
        basis_zero = one_minus * one_minus * one_minus / 6.0
        basis_one = (3.0 * pos_cube - 6.0 * pos_square + 4.0) / 6.0
        basis_two = (-3.0 * pos_cube + 3.0 * pos_square + 3.0 * position + 1.0) / 6.0
        basis_three = pos_cube / 6.0
        basis_value = jnp.where(
            offset == 0,
            basis_zero,
            jnp.where(
                offset == 1,
                basis_one,
                jnp.where(offset == 2, basis_two, jnp.where(offset == 3, basis_three, 0.0)),
            ),
        )
        summed = summed + weight * basis_value
    return summed.astype(jnp.bfloat16)


def on_device(spline_index, spline_frac, projection, forces, row_owner, row_offset):
    row_count = spline_index.shape[0]
    slot_width = spline_index.shape[1]
    device_count = lax.axis_size(("frame", "panel"))
    capacity = max(2, 2 * row_count // device_count)
    slot_count = device_count * capacity
    owners = row_owner[:, 0]
    same_owner = owners[:, None] == owners[None, :]
    order_index = lax.broadcasted_iota(jnp.int32, (row_count, row_count), 0)
    other_index = lax.broadcasted_iota(jnp.int32, (row_count, row_count), 1)
    position = jnp.sum((same_owner & (other_index < order_index)).astype(jnp.int32), axis=1)
    target = owners * capacity + position

    def place(values):
        empty = jnp.zeros((slot_count,) + values.shape[1:], values.dtype)
        return empty.at[target].set(values)

    send_index = place(spline_index)
    send_frac = place(spline_frac)
    send_proj = place(projection)
    send_force = place(forces)
    send_offset = place(row_offset)
    incoming = (
        lax.all_to_all(send_index, ("frame", "panel"), split_axis=0, concat_axis=0, tiled=True),
        lax.all_to_all(send_frac, ("frame", "panel"), split_axis=0, concat_axis=0, tiled=True),
        lax.all_to_all(send_proj, ("frame", "panel"), split_axis=0, concat_axis=0, tiled=True),
        lax.all_to_all(send_force, ("frame", "panel"), split_axis=0, concat_axis=0, tiled=True),
        lax.all_to_all(send_offset, ("frame", "panel"), split_axis=0, concat_axis=0, tiled=True),
    )
    batch_size = 16
    turns = slot_count // batch_size

    def split(member):
        return member.reshape((turns, batch_size) + member.shape[1:])

    def accumulate(totals, pieces):
        band_acc, rhs_acc = totals
        index_part, frac_part, proj_part, force_part, offset_part = pieces
        design = basis_tiles(index_part, frac_part, proj_part, CO)
        for band_lag in range(slot_width):
            left_tiles = design[:, : slot_width - band_lag]
            right_tiles = design[:, band_lag:]
            products = jnp.einsum(
                "bsxi,bsxj->bsij", left_tiles, right_tiles, preferred_element_type=jnp.float32
            )
            rows_at = offset_part[:, None] + lax.broadcasted_iota(
                jnp.int32, (1, slot_width - band_lag), 1
            )
            band_acc = band_acc.at[rows_at, band_lag].add(products)
        moments = jnp.einsum("bsxi,bx->bsi", design, force_part, preferred_element_type=jnp.float32)
        rows_all = offset_part[:, None] + lax.broadcasted_iota(jnp.int32, (1, slot_width), 1)
        rhs_acc = rhs_acc.at[rows_all].add(moments)
        return ((band_acc, rhs_acc), None)

    acc_rows = BLK_DEV + slot_width - 1
    band_init = jnp.zeros((acc_rows, slot_width, CO, CO), jnp.float32)
    rhs_init = jnp.zeros((acc_rows, CO), jnp.float32)
    (band_acc, rhs_acc), unused = lax.scan(
        accumulate,
        (band_init, rhs_init),
        (
            split(incoming[0]),
            split(incoming[1]),
            split(incoming[2]),
            split(incoming[3]),
            split(incoming[4]),
        ),
    )
    spill_band, spill_rhs = shifted((band_acc[BLK_DEV:], rhs_acc[BLK_DEV:]), ("frame", "panel"), 1)
    normal_band = band_acc[:BLK_DEV].at[: slot_width - 1].add(spill_band)
    normal_rhs = rhs_acc[:BLK_DEV].at[: slot_width - 1].add(spill_rhs)
    return (normal_band, normal_rhs)


def solution(mesh):
    in_specs = (
        P(("frame", "panel"), None, None, None),
        P(("frame", "panel"), None, None, None),
        P(("frame", "panel"), None, None, None),
        P(("frame", "panel"), None),
        P(("frame", "panel"), None),
        P(("frame", "panel")),
    )
    out_specs = (P(("frame", "panel"), None, None, None), P(("frame", "panel"), None))
    return jax.shard_map(
        on_device, mesh=mesh, in_specs=in_specs, out_specs=out_specs, check_vma=False
    )
```

profile of v0, /device:TPU:1, one launch (start us, length us, event | category | flops | bytes accessed | tf_op | source)
XLA Modules:
  0.0 853.6 jit_solution(1311963996199205946)
XLA Ops:
  4.1 11.5 %all-to-all-start = ((s32[128,2,1]{1,2,0:T(1,128)}), s32[128,2,1]{1,2,0:T(1,128)S(1)}, u32[]{:S(2)}, u32[]{:S(2)}) async-start(s32[128,2,1]{1,2,0:T(1,128)} %bitcast.34), calls=%async_computation | async-start | bytes 131072 | tf_op jit(solution)/shard_map/all_to_all | solution.py:70
  17.7 7.5 all-to-all-done
  30.8 16.5 %scatter_fusion.3 = bf16[256,2,4,256]{3,2,1,0:T(4,128)(2,1)} fusion(bf16[256,2,4,256]{3,2,1,0:T(4,128)(2,1)} %broadcast.416.clone, s32[128]{0:T(128)S(1)} %fusion.85, bf16[128,2,4,256]{3,2,1,0:T(4,128)(2,1)} %param.14), kind=kCustom, calls=%fused_computation.4 | custom fusion | bytes 1573376 | tf_op jit(solution)/shard_map/scatter | solution.py:58
  47.3 10.2 %all-to-all-start.1 = ((bf16[256,2,4,256]{3,2,1,0:T(4,128)(2,1)}), bf16[256,2,4,256]{3,2,1,0:T(4,128)(2,1)}, u32[]{:S(2)}, u32[]{:S(2)}) async-start(bf16[256,2,4,256]{3,2,1,0:T(4,128)(2,1)} %scatter_fusion.3), calls=%async_computation.1 | async-start | bytes 2097152 | tf_op jit(solution)/shard_map/all_to_all | solution.py:68
  58.8 14.4 %scatter_fusion.5 = bf16[256,2,4,256]{3,2,1,0:T(4,128)(2,1)} fusion(bf16[256,2,4,256]{3,2,1,0:T(4,128)(2,1)} %broadcast.416.clone.1, s32[128]{0:T(128)S(1)} %fusion.85, bf16[128,2,4,256]{3,2,1,0:T(4,128)(2,1)S(1)} %copy-done.5), kind=kCustom, calls=%fused_computation.6 | custom fusion | bytes 1573376 | tf_op jit(solution)/shard_map/scatter | solution.py:58
  76.0 7.3 all-to-all-start.3
  85.0 13.7 %scatter_fusion.4 = s32[256,2,4,256]{3,2,1,0:T(4,128)} fusion(s32[256,2,4,256]{3,2,1,0:T(4,128)} %broadcast_in_dim.124, s32[128]{0:T(128)S(1)} %fusion.85, s32[128,2,4,256]{3,2,1,0:T(4,128)S(1)} %copy-done.4), kind=kCustom, calls=%fused_computation.5 | custom fusion | bytes 3146240 | tf_op jit(solution)/shard_map/scatter | solution.py:58
  110.0 28.9 %all-to-all-done.2 = s32[256,2,4,256]{3,2,1,0:T(4,128)S(1)} async-done(((s32[256,2,4,256]{3,2,1,0:T(4,128)}), s32[256,2,4,256]{3,2,1,0:T(4,128)S(1)}, u32[]{:S(2)}, u32[]{:S(2)}) %all-to-all-start.2) | async-done | bytes 2097184 | tf_op jit(solution)/shard_map/all_to_all | solution.py:66
  140.9 704.3 %while.14 = (s32[]{:T(128)}, f32[23,2,128,128]{3,2,1,0:T(8,128)}, f32[23,128]{1,0:T(8,128)S(1)}, s32[16,16]{1,0:T(8,128)S(1)}, bf16[16,16,2,4,256]{4,3,2,1,0:T(4...) while((s32[]{:T(128)}, f32[23,2,128,128]{3,2,1,0:T(8,128)}, ...), condition=%wide.region_10.11_spmd, body=%wide.region_6.10_spmd.sunk | while | flops 452366784 | bytes 40724592 | solution.py:100
  142.6 27.9 %add_convert_fusion.2 = bf16[16,2,256,128]{3,2,0,1:T(8,128)(2,1)S(1)} fusion(f32[16,2,256]{2,0,1:T(8,128)S(1)} %get-tuple-element.218, f32[16,2,256]{2,0,1:T(8,128)S(1)} %get-tuple-element.219, f32[16,2,256]{2,0,1:T(8,128)S(1)} %get-tuple-element.220, f32[16,2,256]{2,0,1:T(8,128)S(1)} %get-tuple-element.221, s32[16,2,256]{2,0,1:T(8,128)S(1)} %get-tuple-element.222, ...), kind=kLoop, calls=%fused_computation.8.clone.1 | loop fusion | flops 46137344 | bytes 2883584 | tf_op jit(solution)/shard_map/while/body/eval_jaxpr/convert_element_type | solution.py:40
  186.7 27.9 %add_convert_fusion.2 = bf16[16,2,256,128]{3,2,0,1:T(8,128)(2,1)S(1)} fusion(f32[16,2,256]{2,0,1:T(8,128)S(1)} %get-tuple-element.218, f32[16,2,256]{2,0,1:T(8,128)S(1)} %get-tuple-element.219, f32[16,2,256]{2,0,1:T(8,128)S(1)} %get-tuple-element.220, f32[16,2,256]{2,0,1:T(8,128)S(1)} %get-tuple-element.221, s32[16,2,256]{2,0,1:T(8,128)S(1)} %get-tuple-element.222, ...), kind=kLoop, calls=%fused_computation.8.clone.1 | loop fusion | flops 46137344 | bytes 2883584 | tf_op jit(solution)/shard_map/while/body/eval_jaxpr/convert_element_type | solution.py:40
  230.6 27.9 %add_convert_fusion.2 = bf16[16,2,256,128]{3,2,0,1:T(8,128)(2,1)S(1)} fusion(f32[16,2,256]{2,0,1:T(8,128)S(1)} %get-tuple-element.218, f32[16,2,256]{2,0,1:T(8,128)S(1)} %get-tuple-element.219, f32[16,2,256]{2,0,1:T(8,128)S(1)} %get-tuple-element.220, f32[16,2,256]{2,0,1:T(8,128)S(1)} %get-tuple-element.221, s32[16,2,256]{2,0,1:T(8,128)S(1)} %get-tuple-element.222, ...), kind=kLoop, calls=%fused_computation.8.clone.1 | loop fusion | flops 46137344 | bytes 2883584 | tf_op jit(solution)/shard_map/while/body/eval_jaxpr/convert_element_type | solution.py:40
  274.6 27.9 %add_convert_fusion.2 = bf16[16,2,256,128]{3,2,0,1:T(8,128)(2,1)S(1)} fusion(f32[16,2,256]{2,0,1:T(8,128)S(1)} %get-tuple-element.218, f32[16,2,256]{2,0,1:T(8,128)S(1)} %get-tuple-element.219, f32[16,2,256]{2,0,1:T(8,128)S(1)} %get-tuple-element.220, f32[16,2,256]{2,0,1:T(8,128)S(1)} %get-tuple-element.221, s32[16,2,256]{2,0,1:T(8,128)S(1)} %get-tuple-element.222, ...), kind=kLoop, calls=%fused_computation.8.clone.1 | loop fusion | flops 46137344 | bytes 2883584 | tf_op jit(solution)/shard_map/while/body/eval_jaxpr/convert_element_type | solution.py:40
  318.4 27.9 %add_convert_fusion.2 = bf16[16,2,256,128]{3,2,0,1:T(8,128)(2,1)S(1)} fusion(f32[16,2,256]{2,0,1:T(8,128)S(1)} %get-tuple-element.218, f32[16,2,256]{2,0,1:T(8,128)S(1)} %get-tuple-element.219, f32[16,2,256]{2,0,1:T(8,128)S(1)} %get-tuple-element.220, f32[16,2,256]{2,0,1:T(8,128)S(1)} %get-tuple-element.221, s32[16,2,256]{2,0,1:T(8,128)S(1)} %get-tuple-element.222, ...), kind=kLoop, calls=%fused_computation.8.clone.1 | loop fusion | flops 46137344 | bytes 2883584 | tf_op jit(solution)/shard_map/while/body/eval_jaxpr/convert_element_type | solution.py:40
  362.3 27.9 %add_convert_fusion.2 = bf16[16,2,256,128]{3,2,0,1:T(8,128)(2,1)S(1)} fusion(f32[16,2,256]{2,0,1:T(8,128)S(1)} %get-tuple-element.218, f32[16,2,256]{2,0,1:T(8,128)S(1)} %get-tuple-element.219, f32[16,2,256]{2,0,1:T(8,128)S(1)} %get-tuple-element.220, f32[16,2,256]{2,0,1:T(8,128)S(1)} %get-tuple-element.221, s32[16,2,256]{2,0,1:T(8,128)S(1)} %get-tuple-element.222, ...), kind=kLoop, calls=%fused_computation.8.clone.1 | loop fusion | flops 46137344 | bytes 2883584 | tf_op jit(solution)/shard_map/while/body/eval_jaxpr/convert_element_type | solution.py:40
  393.8 7.2 scatter_fusion
  406.3 27.9 %add_convert_fusion.2 = bf16[16,2,256,128]{3,2,0,1:T(8,128)(2,1)S(1)} fusion(f32[16,2,256]{2,0,1:T(8,128)S(1)} %get-tuple-element.218, f32[16,2,256]{2,0,1:T(8,128)S(1)} %get-tuple-element.219, f32[16,2,256]{2,0,1:T(8,128)S(1)} %get-tuple-element.220, f32[16,2,256]{2,0,1:T(8,128)S(1)} %get-tuple-element.221, s32[16,2,256]{2,0,1:T(8,128)S(1)} %get-tuple-element.222, ...), kind=kLoop, calls=%fused_computation.8.clone.1 | loop fusion | flops 46137344 | bytes 2883584 | tf_op jit(solution)/shard_map/while/body/eval_jaxpr/convert_element_type | solution.py:40
  437.9 7.2 scatter_fusion
  450.2 27.9 %add_convert_fusion.2 = bf16[16,2,256,128]{3,2,0,1:T(8,128)(2,1)S(1)} fusion(f32[16,2,256]{2,0,1:T(8,128)S(1)} %get-tuple-element.218, f32[16,2,256]{2,0,1:T(8,128)S(1)} %get-tuple-element.219, f32[16,2,256]{2,0,1:T(8,128)S(1)} %get-tuple-element.220, f32[16,2,256]{2,0,1:T(8,128)S(1)} %get-tuple-element.221, s32[16,2,256]{2,0,1:T(8,128)S(1)} %get-tuple-element.222, ...), kind=kLoop, calls=%fused_computation.8.clone.1 | loop fusion | flops 46137344 | bytes 2883584 | tf_op jit(solution)/shard_map/while/body/eval_jaxpr/convert_element_type | solution.py:40
  481.8 7.2 scatter_fusion
  494.2 27.9 %add_convert_fusion.2 = bf16[16,2,256,128]{3,2,0,1:T(8,128)(2,1)S(1)} fusion(f32[16,2,256]{2,0,1:T(8,128)S(1)} %get-tuple-element.218, f32[16,2,256]{2,0,1:T(8,128)S(1)} %get-tuple-element.219, f32[16,2,256]{2,0,1:T(8,128)S(1)} %get-tuple-element.220, f32[16,2,256]{2,0,1:T(8,128)S(1)} %get-tuple-element.221, s32[16,2,256]{2,0,1:T(8,128)S(1)} %get-tuple-element.222, ...), kind=kLoop, calls=%fused_computation.8.clone.1 | loop fusion | flops 46137344 | bytes 2883584 | tf_op jit(solution)/shard_map/while/body/eval_jaxpr/convert_element_type | solution.py:40
  525.8 7.5 scatter_fusion
  538.8 27.9 %add_convert_fusion.2 = bf16[16,2,256,128]{3,2,0,1:T(8,128)(2,1)S(1)} fusion(f32[16,2,256]{2,0,1:T(8,128)S(1)} %get-tuple-element.218, f32[16,2,256]{2,0,1:T(8,128)S(1)} %get-tuple-element.219, f32[16,2,256]{2,0,1:T(8,128)S(1)} %get-tuple-element.220, f32[16,2,256]{2,0,1:T(8,128)S(1)} %get-tuple-element.221, s32[16,2,256]{2,0,1:T(8,128)S(1)} %get-tuple-element.222, ...), kind=kLoop, calls=%fused_computation.8.clone.1 | loop fusion | flops 46137344 | bytes 2883584 | tf_op jit(solution)/shard_map/while/body/eval_jaxpr/convert_element_type | solution.py:40
  570.4 7.2 scatter_fusion
  582.9 27.9 %add_convert_fusion.2 = bf16[16,2,256,128]{3,2,0,1:T(8,128)(2,1)S(1)} fusion(f32[16,2,256]{2,0,1:T(8,128)S(1)} %get-tuple-element.218, f32[16,2,256]{2,0,1:T(8,128)S(1)} %get-tuple-element.219, f32[16,2,256]{2,0,1:T(8,128)S(1)} %get-tuple-element.220, f32[16,2,256]{2,0,1:T(8,128)S(1)} %get-tuple-element.221, s32[16,2,256]{2,0,1:T(8,128)S(1)} %get-tuple-element.222, ...), kind=kLoop, calls=%fused_computation.8.clone.1 | loop fusion | flops 46137344 | bytes 2883584 | tf_op jit(solution)/shard_map/while/body/eval_jaxpr/convert_element_type | solution.py:40
  614.5 7.4 scatter_fusion
  627.1 27.9 %add_convert_fusion.2 = bf16[16,2,256,128]{3,2,0,1:T(8,128)(2,1)S(1)} fusion(f32[16,2,256]{2,0,1:T(8,128)S(1)} %get-tuple-element.218, f32[16,2,256]{2,0,1:T(8,128)S(1)} %get-tuple-element.219, f32[16,2,256]{2,0,1:T(8,128)S(1)} %get-tuple-element.220, f32[16,2,256]{2,0,1:T(8,128)S(1)} %get-tuple-element.221, s32[16,2,256]{2,0,1:T(8,128)S(1)} %get-tuple-element.222, ...), kind=kLoop, calls=%fused_computation.8.clone.1 | loop fusion | flops 46137344 | bytes 2883584 | tf_op jit(solution)/shard_map/while/body/eval_jaxpr/convert_element_type | solution.py:40
  658.7 7.2 scatter_fusion
  671.1 27.9 %add_convert_fusion.2 = bf16[16,2,256,128]{3,2,0,1:T(8,128)(2,1)S(1)} fusion(f32[16,2,256]{2,0,1:T(8,128)S(1)} %get-tuple-element.218, f32[16,2,256]{2,0,1:T(8,128)S(1)} %get-tuple-element.219, f32[16,2,256]{2,0,1:T(8,128)S(1)} %get-tuple-element.220, f32[16,2,256]{2,0,1:T(8,128)S(1)} %get-tuple-element.221, s32[16,2,256]{2,0,1:T(8,128)S(1)} %get-tuple-element.222, ...), kind=kLoop, calls=%fused_computation.8.clone.1 | loop fusion | flops 46137344 | bytes 2883584 | tf_op jit(solution)/shard_map/while/body/eval_jaxpr/convert_element_type | solution.py:40
  715.0 27.9 %add_convert_fusion.2 = bf16[16,2,256,128]{3,2,0,1:T(8,128)(2,1)S(1)} fusion(f32[16,2,256]{2,0,1:T(8,128)S(1)} %get-tuple-element.218, f32[16,2,256]{2,0,1:T(8,128)S(1)} %get-tuple-element.219, f32[16,2,256]{2,0,1:T(8,128)S(1)} %get-tuple-element.220, f32[16,2,256]{2,0,1:T(8,128)S(1)} %get-tuple-element.221, s32[16,2,256]{2,0,1:T(8,128)S(1)} %get-tuple-element.222, ...), kind=kLoop, calls=%fused_computation.8.clone.1 | loop fusion | flops 46137344 | bytes 2883584 | tf_op jit(solution)/shard_map/while/body/eval_jaxpr/convert_element_type | solution.py:40
  759.0 27.9 %add_convert_fusion.2 = bf16[16,2,256,128]{3,2,0,1:T(8,128)(2,1)S(1)} fusion(f32[16,2,256]{2,0,1:T(8,128)S(1)} %get-tuple-element.218, f32[16,2,256]{2,0,1:T(8,128)S(1)} %get-tuple-element.219, f32[16,2,256]{2,0,1:T(8,128)S(1)} %get-tuple-element.220, f32[16,2,256]{2,0,1:T(8,128)S(1)} %get-tuple-element.221, s32[16,2,256]{2,0,1:T(8,128)S(1)} %get-tuple-element.222, ...), kind=kLoop, calls=%fused_computation.8.clone.1 | loop fusion | flops 46137344 | bytes 2883584 | tf_op jit(solution)/shard_map/while/body/eval_jaxpr/convert_element_type | solution.py:40
  802.9 27.9 %add_convert_fusion.2 = bf16[16,2,256,128]{3,2,0,1:T(8,128)(2,1)S(1)} fusion(f32[16,2,256]{2,0,1:T(8,128)S(1)} %get-tuple-element.218, f32[16,2,256]{2,0,1:T(8,128)S(1)} %get-tuple-element.219, f32[16,2,256]{2,0,1:T(8,128)S(1)} %get-tuple-element.220, f32[16,2,256]{2,0,1:T(8,128)S(1)} %get-tuple-element.221, s32[16,2,256]{2,0,1:T(8,128)S(1)} %get-tuple-element.222, ...), kind=kLoop, calls=%fused_computation.8.clone.1 | loop fusion | flops 46137344 | bytes 2883584 | tf_op jit(solution)/shard_map/while/body/eval_jaxpr/convert_element_type | solution.py:40
  (447 shorter events, 243.6 us)
Async XLA Ops:
  4.1 21.0 %all-to-all-start = ((s32[128,2,1]{1,2,0:T(1,128)}), s32[128,2,1]{1,2,0:T(1,128)S(1)}, u32[]{:S(2)}, u32[]{:S(2)}) async-start(s32[128,2,1]{1,2,0:T(1,128)} %bitcast.34), calls=%async_computation | async-start | bytes 131072 | tf_op jit(solution)/shard_map/all_to_all | solution.py:70
  17.7 41.1 %copy-start.5 = (bf16[128,2,4,256]{3,2,1,0:T(4,128)(2,1)S(1)}, bf16[128,2,4,256]{3,2,1,0:T(4,128)(2,1)}, u32[]{:S(2)}) copy-start(bf16[128,2,4,256]{3,2,1,0:T(4,128)(2,1)} %param.13) | copy-start | bytes 1572868
  25.1 22.1 %all-to-all-start.4 = ((bf16[128,2,256]{2,1,0:T(2,128)(2,1)}), bf16[128,2,256]{2,1,0:T(2,128)(2,1)S(1)}, u32[]{:S(2)}, u32[]{:S(2)}) async-start(bf16[128,2,256]{2,1,0:T(2,128)(2,1)} %all_to_all.26), calls=%async_computation.4 | async-start | bytes 262144 | tf_op jit(solution)/shard_map/all_to_all | solution.py:69
  47.3 28.8 %all-to-all-start.1 = ((bf16[256,2,4,256]{3,2,1,0:T(4,128)(2,1)}), bf16[256,2,4,256]{3,2,1,0:T(4,128)(2,1)}, u32[]{:S(2)}, u32[]{:S(2)}) async-start(bf16[256,2,4,256]{3,2,1,0:T(4,128)(2,1)} %scatter_fusion.3), calls=%async_computation.1 | async-start | bytes 2097152 | tf_op jit(solution)/shard_map/all_to_all | solution.py:68
  58.8 26.2 %copy-start.4 = (s32[128,2,4,256]{3,2,1,0:T(4,128)S(1)}, s32[128,2,4,256]{3,2,1,0:T(4,128)}, u32[]{:S(2)}) copy-start(s32[128,2,4,256]{3,2,1,0:T(4,128)} %param.12) | copy-start | bytes 3145732
  76.0 25.9 %all-to-all-start.3 = ((bf16[256,2,4,256]{3,2,1,0:T(4,128)(2,1)}), bf16[256,2,4,256]{3,2,1,0:T(4,128)(2,1)}, u32[]{:S(2)}, u32[]{:S(2)}) async-start(bf16[256,2,4,256]{3,2,1,0:T(4,128)(2,1)} %scatter_fusion.5), calls=%async_computation.3 | async-start | bytes 2097152 | tf_op jit(solution)/shard_map/all_to_all | solution.py:67
  101.9 37.0 %all-to-all-start.2 = ((s32[256,2,4,256]{3,2,1,0:T(4,128)}), s32[256,2,4,256]{3,2,1,0:T(4,128)S(1)}, u32[]{:S(2)}, u32[]{:S(2)}) async-start(s32[256,2,4,256]{3,2,1,0:T(4,128)} %scatter_fusion.4), calls=%async_computation.2 | async-start | bytes 4194304 | tf_op jit(solution)/shard_map/all_to_all | solution.py:66
  181.3 3.6 copy-start.2
  185.0 1.7 copy-start.1
  225.3 3.5 copy-start.2
  228.9 1.7 copy-start.1
  269.2 3.7 copy-start.2
  272.9 1.7 copy-start.1
  313.2 3.5 copy-start.2
  357.1 3.5 copy-start.2
  360.6 1.7 copy-start.1
  401.0 3.6 copy-start.2
  445.1 3.5 copy-start.2
  489.0 3.5 copy-start.2
  533.3 3.8 copy-start.2
  577.6 3.6 copy-start.2
  621.9 3.5 copy-start.2
  625.4 1.7 copy-start.1
  665.9 3.5 copy-start.2
  709.8 3.5 copy-start.2
  713.3 1.7 copy-start.1
  753.7 3.6 copy-start.2
  797.7 3.5 copy-start.2
  841.6 3.6 copy-start.2
  845.2 3.9 collective-permute-start.1
  849.1 2.0 collective-permute-start
  849.2 2.8 copy-start
  (11 other events, 18.5 us)
where the time goes:
time: 864 us; the launch traced here: 854 us
  other arithmetic  636 us (74%)
  local copies, waits for them, and re-layouts  82.1 us (10%)
  matrix products  47 us (5%)
  waiting for transfers between devices  44.4 us (5%)
  starting transfers between devices  40.9 us (5%)
    convert_element_type x16, other arithmetic, basis_tiles(): return summed.astype(jnp.bfloat16)  446 us
    scatter-add x32, other arithmetic, accumulate(): band_acc = band_acc.at[rows_at, band_lag].add(products)  172 us
    scatter x5, local copies, waits for them, and re-layouts, place(): return empty.at[target].set(values)  47 us
    dot_general x32, matrix products, accumulate(): jnp.einsum('bsxi,bsxj->bsij', left_tiles, right_tiles, preferred_element_...  40.9 us
    all_to_all x1, waiting for transfers between devices, on_device(): lax.all_to_all(send_index, ('frame', 'panel'), split_axis=0, concat_axis=...  28.9 us
    dynamic_slice x80, local copies, waits for them, and re-layouts, on_device(): lax.scan(accumulate, (band_init, rhs_init), (split(incoming[0]), split(in...  18.8 us
  transfers between devices with their start and end apart: 7, of which 5 were waited for; matrix products, arithmetic and copies ran while one was open for 6% of the time, Pallas kernels for 0%

commit v1 on v0

v1 whole, which is shorter than its diff:
```python
import jax
import jax.numpy as jnp
from jax import lax
from jax.experimental import pallas as pl
from jax.experimental.pallas import tpu as pltpu
from jax.sharding import PartitionSpec as P

CO = 128
BLK_DEV = 22
CAP = 2
AXES = ("frame", "panel")
BF16 = jnp.bfloat16
F32 = jnp.float32


def pack_kernel(owner_ref, index_ref, frac_ref, proj_ref, force_ref, out_ref, count_ref, force_buf):
    device_count = out_ref.shape[0]

    @pl.loop(0, device_count)
    def _(d):
        count_ref[d] = 0

    force_buf[...] = force_ref[...].astype(F32)

    @pl.loop(0, owner_ref.shape[0])
    def _(t):
        owner = owner_ref[t]
        place = count_ref[owner]
        count_ref[owner] = place + 1
        for a, ref in enumerate((index_ref, frac_ref, proj_ref)):
            for g in range(2):
                low = ref[t, 0, :, g * 128 : g * 128 + 128].astype(F32)
                high = ref[t, 1, :, g * 128 : g * 128 + 128].astype(F32)
                both = jnp.concatenate([low, high], axis=0).astype(BF16)
                out_ref[owner, place * 6 + a * 2 + g] = both

        row = force_buf[pl.ds(t, 1), :]
        for g in range(2):
            piece = jnp.broadcast_to(row[:, g * 128 : g * 128 + 128], (8, 128)).astype(BF16)
            which = lax.broadcasted_iota(jnp.int32, (8, 128), 0)
            old = out_ref[owner, 12]
            out_ref[owner, 12] = jnp.where(which == place * 2 + g, piece.astype(F32), old.astype(F32)).astype(BF16)


def pack(owners, spline_index, spline_frac, projection, forces, device_count):
    vmem = pl.BlockSpec(memory_space=pltpu.VMEM)
    return pl.pallas_call(
        pack_kernel,
        out_shape=jax.ShapeDtypeStruct((device_count, 13, 8, 128), BF16),
        in_specs=[pl.BlockSpec(memory_space=pltpu.SMEM), vmem, vmem, vmem, vmem],
        out_specs=vmem,
        scratch_shapes=[pltpu.SMEM((device_count,), jnp.int32), pltpu.VMEM(forces.shape, F32)],
        compiler_params=pltpu.CompilerParams(vmem_limit_bytes=40 << 20),
        name="pack",
    )(owners, spline_index, spline_frac, projection, forces)


def spline_rows(recv_ref, source, place, value_buf):
    for g in range(2):
        index = recv_ref[source, place * 6 + g].astype(F32).astype(jnp.int32)
        t = recv_ref[source, place * 6 + 2 + g].astype(F32)
        q = recv_ref[source, place * 6 + 4 + g].astype(F32) * (1.0 / 6.0)
        u = 1.0 - t
        t2 = t * t
        value_buf[0, g] = q * (u * u * u)
        value_buf[1, g] = q * (3.0 * (t2 * t) - 6.0 * t2 + 4.0)
        value_buf[2, g] = q * (3.0 * (t + t2 - t2 * t) + 1.0)
        value_buf[3, g] = q * (t2 * t)
        value_buf[4, g] = (index & 15).astype(F32)
        value_buf[5, g] = (index >> 4).astype(F32)


def build_design(value_buf, design_buf):
    column = lax.broadcasted_iota(jnp.int32, (16, 128), 0).astype(F32).astype(BF16)
    zero = jnp.zeros((16, 128), BF16)

    def spread(k, row, g):
        part = value_buf[k, g, pl.ds(row, 8, stride=0), :]
        return jnp.concatenate([part, part], axis=0).astype(BF16)

    for s in range(2):
        for g in range(2):
            blocks = [None] * 8
            for n in range(4):
                row = s * 4 + n
                low = spread(4, row, g)
                high = spread(5, row, g)
                offset = column - low
                wraps = offset < 0
                offset = jnp.where(wraps, offset + 16, offset)
                home = jnp.where(wraps, high + 1, high)
                window = zero
                for m in range(4):
                    window = jnp.where(offset == m, spread(m, row, g), window)
                for b in range(8):
                    piece = jnp.where(home == b, window, zero)
                    blocks[b] = piece if n == 0 else blocks[b] + piece
            for b in range(8):
                design_buf[s * 128 + b * 16 : s * 128 + b * 16 + 16, g * 128 : g * 128 + 128] = blocks[b]


def force_rows(recv_ref, source, place, design_buf, force_buf):
    force_buf[...] = recv_ref[source, 12].astype(F32)
    first = lax.broadcasted_iota(jnp.int32, (16, 128), 0) == 0
    for g in range(2):
        row = force_buf[pl.ds(place * 2 + g, 8, stride=0), :]
        row = jnp.concatenate([row, row], axis=0)
        design_buf[256:272, g * 128 : g * 128 + 128] = jnp.where(first, row, 0.0).astype(BF16)


def tile_products(recv_ref, code, value_buf, design_buf, force_buf):
    source = code >> 1
    place = code & 1
    spline_rows(recv_ref, source, place, value_buf)
    build_design(value_buf, design_buf)
    force_rows(recv_ref, source, place, design_buf, force_buf)
    return lax.dot_general(
        design_buf[...], design_buf[0:256, :], (((1,), (1,)), ((), ())), preferred_element_type=F32
    )


def edge_kernel(bounds_ref, order_ref, recv_ref, band_ref, rhs_ref, spill_ref, value_buf, design_buf, force_buf):
    band_ref[...] = jnp.zeros_like(band_ref)
    rhs_ref[...] = jnp.zeros_like(rhs_ref)
    spill_ref[...] = jnp.zeros_like(spill_ref)

    @pl.loop(0, bounds_ref[0])
    def _(i):
        out = tile_products(recv_ref, order_ref[i], value_buf, design_buf, force_buf)
        band_ref[0] += out[0:128, 0:128]
        band_ref[1] += out[0:128, 128:256]
        spill_ref[0:128, :] += out[128:256, 128:256]
        rhs_ref[...] += out[256:264, 0:128]
        spill_ref[128:136, :] += out[256:264, 128:256]


def inner_kernel(
    bounds_ref, order_ref, offset_ref, recv_ref, edge_band_ref, edge_rhs_ref, band_ref, rhs_ref,
    value_buf, design_buf, force_buf,
):
    last = band_ref.shape[0] - 1
    band_ref[0:last] = jnp.zeros((last, 2, 128, 128), F32)
    band_ref[last] = edge_band_ref[...]
    rhs_ref[0:last] = jnp.zeros((last, 128), F32)
    rhs_ref[last:last + 1] = edge_rhs_ref[0:1, :]

    @pl.loop(bounds_ref[0], bounds_ref[1])
    def _(i):
        out = tile_products(recv_ref, order_ref[i], value_buf, design_buf, force_buf)
        at = offset_ref[i]
        band_ref[at, 0] += out[0:128, 0:128]
        band_ref[at, 1] += out[0:128, 128:256]
        band_ref[at + 1, 0] += out[128:256, 128:256]
        rhs_ref[pl.ds(at, 1), :] += out[256:257, 0:128]
        rhs_ref[pl.ds(at + 1, 1), :] += out[256:257, 128:256]


SCRATCH = (
    pltpu.VMEM((6, 2, 8, 128), F32),
    pltpu.VMEM((272, 256), BF16),
    pltpu.VMEM((8, 128), F32),
)


def edge(bounds, order, received):
    vmem = pl.BlockSpec(memory_space=pltpu.VMEM)
    smem = pl.BlockSpec(memory_space=pltpu.SMEM)
    return pl.pallas_call(
        edge_kernel,
        out_shape=(
            jax.ShapeDtypeStruct((2, 128, 128), F32),
            jax.ShapeDtypeStruct((8, 128), F32),
            jax.ShapeDtypeStruct((136, 128), F32),
        ),
        in_specs=[smem, smem, vmem],
        out_specs=(vmem, vmem, vmem),
        scratch_shapes=list(SCRATCH),
        compiler_params=pltpu.CompilerParams(vmem_limit_bytes=40 << 20),
        cost_estimate=pl.CostEstimate(flops=4 << 30, bytes_accessed=4 << 20, transcendentals=0),
        name="edge",
    )(bounds, order, received)


def inner(bounds, order, offsets, received, edge_band, edge_rhs):
    vmem = pl.BlockSpec(memory_space=pltpu.VMEM)
    smem = pl.BlockSpec(memory_space=pltpu.SMEM)
    return pl.pallas_call(
        inner_kernel,
        out_shape=(
            jax.ShapeDtypeStruct((BLK_DEV, 2, 128, 128), F32),
            jax.ShapeDtypeStruct((BLK_DEV, 128), F32),
        ),
        in_specs=[smem, smem, smem, vmem, vmem, vmem],
        out_specs=(vmem, vmem),
        scratch_shapes=list(SCRATCH),
        compiler_params=pltpu.CompilerParams(vmem_limit_bytes=40 << 20),
        cost_estimate=pl.CostEstimate(flops=4 << 30, bytes_accessed=4 << 20, transcendentals=0),
        name="inner",
    )(bounds, order, offsets, received, edge_band, edge_rhs)


def work_list(all_owners, all_offsets, me):
    mine = all_owners == me
    before = jnp.cumsum(mine.astype(jnp.int32), axis=1)
    columns = []
    for place in range(CAP):
        here = mine & (before == place + 1)
        columns.append(jnp.sum(jnp.where(here, all_offsets + 1, 0), axis=1))
    slot_offset = jnp.stack(columns, axis=1).reshape(-1) - 1
    count = slot_offset.shape[0]
    key = jnp.where(slot_offset < 0, BLK_DEV, jnp.where(slot_offset == BLK_DEV - 1, -1, slot_offset))
    ahead = lax.broadcasted_iota(jnp.int32, (count, count), 1) < lax.broadcasted_iota(jnp.int32, (count, count), 0)
    smaller = (key[None, :] < key[:, None]) | ((key[None, :] == key[:, None]) & ahead)
    rank = jnp.sum(smaller.astype(jnp.int32), axis=1)
    chosen = rank[None, :] == lax.broadcasted_iota(jnp.int32, (count, count), 0)
    order = jnp.sum(jnp.where(chosen, lax.broadcasted_iota(jnp.int32, (count, count), 1), 0), axis=1)
    offsets = jnp.sum(jnp.where(chosen, slot_offset[None, :], 0), axis=1)
    bounds = jnp.stack([jnp.sum((slot_offset == BLK_DEV - 1).astype(jnp.int32)), jnp.sum((slot_offset >= 0).astype(jnp.int32))])
    return bounds, order, offsets


def on_device(spline_index, spline_frac, projection, forces, row_owner, row_offset):
    device_count = lax.axis_size(AXES)
    owners = row_owner[:, 0]
    sent = pack(owners, spline_index, spline_frac, projection, forces, device_count)
    received = lax.all_to_all(sent, AXES, split_axis=0, concat_axis=0, tiled=True)
    meta = lax.all_gather(jnp.stack([owners, row_offset]), AXES)
    bounds, order, offsets = work_list(meta[:, 0], meta[:, 1], lax.axis_index(AXES))
    edge_band, edge_rhs, spill = edge(bounds, order, received)
    route = [(i, (i + 1) % device_count) for i in range(device_count)]
    spill = lax.ppermute(spill, AXES, route)
    band, rhs = inner(bounds, order, offsets, received, edge_band, edge_rhs)
    band = band.at[0, 0].add(spill[0:128])
    rhs = rhs.at[0].add(spill[128])
    return band, rhs


def solution(mesh):
    in_specs = (
        P(AXES, None, None, None),
        P(AXES, None, None, None),
        P(AXES, None, None, None),
        P(AXES, None),
        P(AXES, None),
        P(AXES),
    )
    out_specs = (P(AXES, None, None, None), P(AXES, None))
    return jax.shard_map(
        on_device, mesh=mesh, in_specs=in_specs, out_specs=out_specs, check_vma=False
    )
```

time: 864 us -> 144 us (0.17); the launches traced: 854 us -> 143 us
  other arithmetic: 636 us -> 6.24 us
  local copies, waits for them, and re-layouts: 82.1 us -> 8.09 us
  blocking collectives: 0 us -> 68.1 us
  Pallas kernels: 0 us -> 48.7 us
  matrix products: 47 us -> 0 us
  waiting for transfers between devices: 44.4 us -> 0.01 us
  starting transfers between devices: 40.9 us -> 11.6 us
    convert_element_type x32 -> x1, other arithmetic: 447 us -> 0.64 us  [work_list(): before = jnp.cumsum(mine.astype(jnp.int32), axis=1)]
    scatter-add x49 -> x1, other arithmetic: 184 us -> 1.48 us  [on_device(): band = band.at[0, 0].add(spill[0:128])]
    all_gather x0 -> x1, blocking collectives: none -> 68.1 us  [on_device(): meta = lax.all_gather(jnp.stack([owners, row_offset]), AXES)]
    pallas_call x0 -> x3, Pallas kernels: none -> 48.7 us  [the longest x1 21.5 us: edge(): pl.pallas_call(edge_kernel, out_shape=(jax.ShapeDtypeStruct((2, 128, 128)...]
    scatter x5 -> x0, local copies, waits for them, and re-layouts: 47 us -> none  [place(): return empty.at[target].set(values)]
    dot_general x48 -> x0, matrix products: 47 us -> none  [the longest x32 40.9 us: accumulate(): jnp.einsum('bsxi,bsxj->bsij', left_tiles, right_tiles, preferred_element_...]
    all_to_all x5 -> x1, waiting for transfers between devices: 42.5 us -> 0.01 us  [on_device(): lax.all_to_all(sent, AXES, split_axis=0, concat_axis=0, tiled=True)]
    all_to_all x5 -> x1, starting transfers between devices: 39.9 us -> 11.5 us  [on_device(): lax.all_to_all(sent, AXES, split_axis=0, concat_axis=0, tiled=True)]
  transfers between devices with their start and end apart: 7 -> 2, of which waited for: 5 -> 0; matrix products, arithmetic and copies ran while one was open for 6% -> 4% of each run, Pallas kernels for 0% -> 15%
where the time goes in v1:
time: 144 us; the launch traced here: 143 us
  blocking collectives  68.1 us (47%)
  Pallas kernels  48.7 us (34%)
  starting transfers between devices  11.6 us (8%)
  local copies, waits for them, and re-layouts  8.09 us (6%)
  other arithmetic  6.24 us (4%)
    all_gather x1, blocking collectives, on_device(): meta = lax.all_gather(jnp.stack([owners, row_offset]), AXES)  68.1 us
    pallas_call x1, Pallas kernels, edge(): pl.pallas_call(edge_kernel, out_shape=(jax.ShapeDtypeStruct((2, 128, 128)...  21.5 us
    pallas_call x1, Pallas kernels, inner(): pl.pallas_call(inner_kernel, out_shape=(jax.ShapeDtypeStruct((BLK_DEV, 2,...  21.4 us
    all_to_all x1, starting transfers between devices, on_device(): lax.all_to_all(sent, AXES, split_axis=0, concat_axis=0, tiled=True)  11.5 us
    unnamed x16, local copies, waits for them, and re-layouts  5.82 us
    pallas_call x1, Pallas kernels, pack(): pl.pallas_call(pack_kernel, out_shape=jax.ShapeDtypeStruct((device_count,...  5.79 us
  transfers between devices with their start and end apart: 2, of which 0 were waited for; matrix products, arithmetic and copies ran while one was open for 4% of the time, Pallas kernels for 15%

profile of v1, /device:TPU:1, one launch (start us, length us, event | category | flops | bytes accessed | tf_op | source)
XLA Modules:
  0.0 143.4 jit_solution(4614955142802674265)
XLA Ops:
  0.6 0.0 copy-start
  0.6 1.2 copy-done
  1.9 0.0 copy-start.1
  1.9 1.0 copy-done.1
  2.9 0.0 copy-start.2
  2.9 1.0 copy-done.2
  3.9 0.8 copy-done.3
  4.8 0.7 copy-done.4
  5.4 5.8 %pack.1 = bf16[128,13,8,128]{3,2,1,0:T(8,128)(2,1)} custom-call(s32[128]{0:T(128)S(1)} %bitcast.30, s32[128,2,4,256]{3,2,1,0:T(4,128)S(1)} %copy-done, bf16[128,2,4,256]{3,2,1,0:T(4,128)(2,1)S(1)} %copy-done.1, bf16[128,2,4,256]{3,2,1,0:T(4,128)(2,1)S(1)} %copy-done.2, bf16[128,256]{1,0:T(8,128)(2,1)S(1)} %copy-done.3), custom_call_target="tpu_custom_call" | custom-call | tf_op jit(solution)/shard_map/pack/pallas_call | solution.py:47
  11.2 11.5 %all-to-all-start = ((bf16[128,13,8,128]{3,2,1,0:T(8,128)(2,1)}), bf16[128,13,8,128]{3,2,1,0:T(8,128)(2,1)S(1)}, u32[]{:S(2)}, u32[]{:S(2)}) async-start(bf16[128,13,8,128]{3,2,1,0:T(8,128)(2,1)} %pack.1), calls=%async_computation | async-start | bytes 6815744 | tf_op jit(solution)/shard_map/all_to_all | solution.py:226
  22.7 0.0 copy-done.5
  22.7 0.0 copy-done.6
  22.8 68.1 %all-gather.1 = s32[128,2,128]{2,1,0:T(2,128)S(1)} all-gather(s32[1,2,128]{2,1,0:T(2,128)S(1)} %add_bitcast_fusion), channel_id=2, replica_groups=mesh['frame'=4,'panel'=32] {'frame','panel'}, dimensions={0}, use_global_device_ids=true | all-gather | bytes 132096 | tf_op jit(solution)/shard_map/all_gather | solution.py:227
  90.8 0.7 fusion.8
  91.6 0.1 copy.17
  91.7 0.9 copy.16
  92.6 0.6 bitcast_convert_fusion
  93.2 1.0 reduce_window_sum.11
  94.3 0.6 fusion.6
  94.9 0.1 copy.15
  95.1 0.1 sub.7
  95.2 1.4 pad_add_fusion.bounds_ref
  96.6 0.2 convert_reduce_fusion
  96.8 0.2 select_reduce_fusion
  96.9 0.0 all-to-all-done.recv_ref
  96.9 21.5 %edge.1 = (f32[2,128,128]{2,1,0:T(8,128)S(1)}, f32[8,128]{1,0:T(8,128)S(1)}, f32[136,128]{1,0:T(8,128)S(1)}) custom-call(s32[2]{0:T(128)S(1)} %pad_add_fusion.bounds_ref, s32[256]{0:T(256)S(1)} %get-tuple-element.39.order_ref, bf16[128,13,8,128]{3,2,1,0:T(8,128)(2,1)S(1)} %all-to-all-done.recv_ref), custom_call_target="tpu_custom_call" | custom-call | flops 4294967296 | bytes 4194304 | tf_op jit(solution)/shard_map/edge/pallas_call | solution.py:168
  118.5 0.1 collective-permute-start
  118.5 21.4 %inner.1 = (f32[22,2,128,128]{3,2,1,0:T(8,128)}, f32[22,128]{1,0:T(8,128)}) custom-call(s32[2]{0:T(128)S(1)} %pad_add_fusion.bounds_ref, s32[256]{0:T(256)S(1)} %get-tuple-element.39.order_ref, s32[256]{0:T(256)S(1)} %get-tuple-element.38.offset_ref, bf16[128,13,8,128]{3,2,1,0:T(8,128)(2,1)S(1)} %all-to-all-done.recv_ref, ...), custom_call_target="tpu_custom_call" | custom-call | flops 4294967296 | bytes 4194304 | tf_op jit(solution)/shard_map/inner/pallas_call | solution.py:187
  139.9 0.0 collective-permute-done
  139.9 0.7 slice_add_fusion
  140.6 1.3 scatter-add.9
  141.9 1.5 %fusion.3 = f32[22,2,128,128]{3,2,1,0:T(8,128)} fusion(f32[22,2,128,128]{3,2,1,0:T(8,128)} %get-tuple-element.33, f32[136,128]{1,0:T(8,128)S(1)} %collective-permute-done), kind=kLoop, calls=%fused_computation.9 | loop fusion | flops 16384 | bytes 196608 | tf_op jit(solution)/shard_map/scatter-add | solution.py:233
  (7 shorter events, 0.1 us)
Async XLA Ops:
  0.6 1.2 copy-start
  1.9 1.0 copy-start.1
  2.9 1.0 copy-start.2
  3.9 0.8 copy-start.3
  4.8 0.7 copy-start.4
  11.2 11.5 %copy-start.5 = (s32[128,1]{0,1:T(1,128)S(1)}, s32[128,1]{0,1:T(1,128)}, u32[]{:S(2)}) copy-start(s32[128,1]{0,1:T(1,128)} %param.14) | copy-start | bytes 1540
  11.2 11.5 %copy-start.6 = (s32[128]{0:T(128)S(1)}, s32[128]{0:T(128)}, u32[]{:S(2)}) copy-start(s32[128]{0:T(128)} %param.15) | copy-start | bytes 1540
  11.2 85.7 %all-to-all-start = ((bf16[128,13,8,128]{3,2,1,0:T(8,128)(2,1)}), bf16[128,13,8,128]{3,2,1,0:T(8,128)(2,1)S(1)}, u32[]{:S(2)}, u32[]{:S(2)}) async-start(bf16[128,13,8,128]{3,2,1,0:T(8,128)(2,1)} %pack.1), calls=%async_computation | async-start | bytes 6815744 | tf_op jit(solution)/shard_map/all_to_all | solution.py:226
  118.5 21.5 %collective-permute-start = (f32[136,128]{1,0:T(8,128)S(1)}, f32[136,128]{1,0:T(8,128)S(1)}, u32[]{:S(2)}, u32[]{:S(2)}) collective-permute-start(f32[136,128]{1,0:T(8,128)S(1)} %get-tuple-element.34), channel_id=1, source_target_pairs={{0,1},{1,2},{2,3},{3,4},{4,5},{5,6},{6,7},{7,8},{8,9},{9,10},{10,1... | collective-permute-start | bytes 208904 | tf_op jit(solution)/shard_map/ppermute | solution.py:231

commit v2 on v1

v2 whole, which is shorter than its diff:
```python
import jax
import jax.numpy as jnp
from jax import lax
from jax.experimental import pallas as pl
from jax.experimental.pallas import tpu as pltpu
from jax.sharding import PartitionSpec as P

CO = 128
BLK_DEV = 22
CAP = 2
AXES = ("frame", "panel")
BF16 = jnp.bfloat16
F32 = jnp.float32
CHUNKS = 8
MiB = 1 << 20


def pack_kernel(
    owner_ref, offset_ref, me_ref, index_hbm, frac_hbm, proj_hbm, force_hbm, out_hbm,
    count_ref, index_ref, frac_ref, proj_ref, force_ref, force_f32, tile_ref, tail_f32, tail_ref,
    in_sems, force_sem, out_sem, tail_sem,
):
    device_count = out_hbm.shape[0]
    tiles = owner_ref.shape[0]
    step = tiles // CHUNKS
    arrays = ((index_hbm, index_ref), (frac_hbm, frac_ref), (proj_hbm, proj_ref))

    def fetch(a, c):
        part = pl.ds(c * step, step)
        return pltpu.make_async_copy(arrays[a][0].at[part], arrays[a][1].at[part], in_sems.at[a, c])

    force_copy = pltpu.make_async_copy(force_hbm, force_ref, force_sem)
    force_copy.start()
    for c in range(CHUNKS):
        for a in range(3):
            fetch(a, c).start()

    @pl.loop(0, device_count, unroll=8)
    def _(d):
        count_ref[d] = 0

    tail_f32[...] = jnp.zeros_like(tail_f32)
    here = lax.broadcasted_iota(jnp.int32, (1, 128), 1) == me_ref[0]
    force_copy.wait()
    force_f32[...] = force_ref[...].astype(F32)

    for c in range(CHUNKS):
        for a in range(3):
            fetch(a, c).wait()

        @pl.loop(c * step, (c + 1) * step, unroll=2)
        def _(t):
            owner = owner_ref[t]
            place = count_ref[owner]
            count_ref[owner] = place + 1
            for a in range(3):
                ref = arrays[a][1]
                for g in range(2):
                    low = ref[t, 0, :, g * 128 : g * 128 + 128].astype(F32)
                    high = ref[t, 1, :, g * 128 : g * 128 + 128].astype(F32)
                    tile_ref[t, a * 2 + g] = jnp.concatenate([low, high], axis=0).astype(BF16)
            pltpu.make_async_copy(tile_ref.at[t], out_hbm.at[owner, pl.ds(place * 6, 6)], out_sem).start()
            row = force_f32[pl.ds(t, 1), :]
            for g in range(2):
                tail_f32[owner, pl.ds(place * 2 + g, 1), :] = row[:, g * 128 : g * 128 + 128]
            tail_f32[owner, pl.ds(4 + place, 1), :] = jnp.where(here, (offset_ref[t] + 1).astype(F32), 0.0)

    tail_ref[...] = tail_f32[...].astype(BF16)
    tail_copy = pltpu.make_async_copy(tail_ref, out_hbm.at[:, 12], tail_sem)
    tail_copy.start()
    tail_copy.wait()
    pltpu.make_async_copy(tile_ref, tile_ref, out_sem).wait()


def pack(owners, offsets, me, spline_index, spline_frac, projection, forces, device_count):
    hbm = pl.BlockSpec(memory_space=pltpu.HBM)
    smem = pl.BlockSpec(memory_space=pltpu.SMEM)
    tiles = owners.shape[0]
    return pl.pallas_call(
        pack_kernel,
        out_shape=jax.ShapeDtypeStruct((device_count, 13, 8, 128), BF16),
        in_specs=[smem, smem, smem, hbm, hbm, hbm, hbm],
        out_specs=hbm,
        scratch_shapes=[
            pltpu.SMEM((device_count,), jnp.int32),
            pltpu.VMEM(spline_index.shape, spline_index.dtype),
            pltpu.VMEM(spline_frac.shape, BF16),
            pltpu.VMEM(projection.shape, BF16),
            pltpu.VMEM(forces.shape, BF16),
            pltpu.VMEM(forces.shape, F32),
            pltpu.VMEM((tiles, 6, 8, 128), BF16),
            pltpu.VMEM((device_count, 8, 128), F32),
            pltpu.VMEM((device_count, 8, 128), BF16),
            pltpu.SemaphoreType.DMA((3, CHUNKS)),
            pltpu.SemaphoreType.DMA,
            pltpu.SemaphoreType.DMA,
            pltpu.SemaphoreType.DMA,
        ],
        compiler_params=pltpu.CompilerParams(vmem_limit_bytes=40 * MiB),
        name="pack",
    )(owners, offsets, me, spline_index, spline_frac, projection, forces)


def spline_rows(recv_ref, source, place, scale, value_buf):
    for g in range(2):
        index = recv_ref[source, place * 6 + g].astype(F32).astype(jnp.int32)
        t = recv_ref[source, place * 6 + 2 + g].astype(F32)
        q = recv_ref[source, place * 6 + 4 + g].astype(F32) * scale
        u = 1.0 - t
        t2 = t * t
        t3 = t2 * t
        value_buf[0, g] = q * (u * u * u)
        value_buf[1, g] = q * (3.0 * t3 - 6.0 * t2 + 4.0)
        value_buf[2, g] = q * (3.0 * (t + t2 - t3) + 1.0)
        value_buf[3, g] = q * t3
        value_buf[4, g] = (index & 15).astype(F32)
        value_buf[5, g] = (index >> 4).astype(F32)


def build_design(value_buf, design_buf):
    column = lax.broadcasted_iota(jnp.int32, (16, 128), 0).astype(F32).astype(BF16)
    zero = jnp.zeros((16, 128), BF16)

    def spread(k, row, g):
        part = value_buf[k, g, pl.ds(row, 8, stride=0), :]
        return jnp.concatenate([part, part], axis=0).astype(BF16)

    for s in range(2):
        for g in range(2):
            blocks = [None] * 8
            for n in range(4):
                row = s * 4 + n
                low = spread(4, row, g)
                high = spread(5, row, g)
                offset = column - low
                wraps = offset < 0
                offset = jnp.where(wraps, offset + 16, offset)
                home = jnp.where(wraps, high + 1, high)
                window = zero
                for m in range(4):
                    window = jnp.where(offset == m, spread(m, row, g), window)
                for b in range(8):
                    piece = jnp.where(home == b, window, zero)
                    blocks[b] = piece if n == 0 else blocks[b] + piece
            for b in range(8):
                design_buf[s * 128 + b * 16 : s * 128 + b * 16 + 16, g * 128 : g * 128 + 128] = blocks[b]


def force_rows(recv_ref, source, place, design_buf, force_buf):
    force_buf[...] = recv_ref[source, 12].astype(F32)
    first = lax.broadcasted_iota(jnp.int32, (16, 128), 0) == 0
    for g in range(2):
        row = force_buf[pl.ds(place * 2 + g, 8, stride=0), :]
        row = jnp.concatenate([row, row], axis=0)
        design_buf[256:272, g * 128 : g * 128 + 128] = jnp.where(first, row, 0.0).astype(BF16)


def build_tile(recv_ref, code, scale, bufs):
    value_buf, design_buf, force_buf = bufs
    source = code >> 1
    place = code & 1
    spline_rows(recv_ref, source, place, scale, value_buf)
    force_rows(recv_ref, source, place, design_buf, force_buf)
    build_design(value_buf, design_buf)


def products(design_buf):
    return lax.dot_general(
        design_buf[...], design_buf[0:256, :], (((1,), (1,)), ((), ())), preferred_element_type=F32
    )


def sweep(first, last, code_at, recv_ref, add, even, odd):
    odd[1][...] = jnp.zeros_like(odd[1])

    def pair(j, carry):
        i = first + 2 * j
        add(jnp.maximum(i - 1, first), products(odd[1]))
        build_tile(recv_ref, code_at(i), 1.0 / 6.0, even)
        add(i, products(even[1]))
        after = jnp.minimum(i + 1, last - 1)
        build_tile(recv_ref, code_at(after), jnp.where(i + 1 < last, 1.0 / 6.0, 0.0).astype(F32), odd)
        return carry

    lax.fori_loop(0, (last - first + 1) // 2, pair, 0)

    @pl.when(last > first)
    def _():
        add(last - 1, products(odd[1]))


def edge_kernel(recv_ref, band_ref, rhs_ref, spill_ref, list_ref, bound_ref, meta_f32, meta_i32, meta_ref, meta_sem, *bufs):
    total = jnp.zeros((8, 128), F32)
    for d in range(recv_ref.shape[0]):
        total = total + recv_ref[d, 12].astype(F32)
    meta_i32[...] = total.astype(jnp.int32)
    meta_copy = pltpu.make_async_copy(meta_i32, meta_ref, meta_sem)
    meta_copy.start()
    band_ref[...] = jnp.zeros_like(band_ref)
    rhs_ref[...] = jnp.zeros_like(rhs_ref)
    spill_ref[...] = jnp.zeros_like(spill_ref)
    meta_copy.wait()

    def scan(d, counts):
        edges, others = counts
        for q in range(CAP):
            mark = meta_ref[4 + q, d]
            list_ref[0, edges] = d * CAP + q
            edges = edges + (mark == BLK_DEV).astype(jnp.int32)
            list_ref[1, others] = d * CAP + q
            list_ref[2, others] = mark - 1
            others = others + ((mark > 0) & (mark < BLK_DEV)).astype(jnp.int32)
        return edges, others

    edges, others = lax.fori_loop(0, recv_ref.shape[0], scan, (0, 0), unroll=8)
    bound_ref[0] = others

    def add(i, out):
        band_ref[0] += out[0:128, 0:128]
        band_ref[1] += out[0:128, 128:256]
        spill_ref[0:128, :] += out[128:256, 128:256]
        rhs_ref[...] += out[256:264, 0:128]
        spill_ref[128:136, :] += out[256:264, 128:256]

    sweep(0, edges, lambda i: list_ref[0, i], recv_ref, add, bufs[0:3], bufs[3:6])


def inner_kernel(bound_ref, list_ref, recv_ref, edge_band_ref, edge_rhs_ref, band_ref, rhs_ref, *bufs):
    last = band_ref.shape[0] - 1
    band_ref[0:last] = jnp.zeros((last, 2, 128, 128), F32)
    band_ref[last] = edge_band_ref[...]
    rhs_ref[0:last] = jnp.zeros((last, 128), F32)
    rhs_ref[last:last + 1] = edge_rhs_ref[0:1, :]

    def add(i, out):
        at = list_ref[2, i]
        band_ref[at, 0] += out[0:128, 0:128]
        band_ref[at, 1] += out[0:128, 128:256]
        band_ref[at + 1, 0] += out[128:256, 128:256]
        rhs_ref[pl.ds(at, 1), :] += out[256:257, 0:128]
        rhs_ref[pl.ds(at + 1, 1), :] += out[256:257, 128:256]

    sweep(0, bound_ref[0], lambda i: list_ref[1, i], recv_ref, add, bufs[0:3], bufs[3:6])


def buffers():
    return [pltpu.VMEM((6, 2, 8, 128), F32), pltpu.VMEM((272, 256), BF16), pltpu.VMEM((8, 128), F32)] * 2


def edge(received):
    vmem = pl.BlockSpec(memory_space=pltpu.VMEM)
    smem = pl.BlockSpec(memory_space=pltpu.SMEM)
    slots = received.shape[0] * CAP
    return pl.pallas_call(
        edge_kernel,
        out_shape=(
            jax.ShapeDtypeStruct((2, 128, 128), F32),
            jax.ShapeDtypeStruct((8, 128), F32),
            jax.ShapeDtypeStruct((136, 128), F32),
            jax.ShapeDtypeStruct((3, slots + 1), jnp.int32),
            jax.ShapeDtypeStruct((1,), jnp.int32),
        ),
        in_specs=[vmem],
        out_specs=(vmem, vmem, vmem, smem, smem),
        scratch_shapes=[
            pltpu.VMEM((8, 128), F32),
            pltpu.VMEM((8, 128), jnp.int32),
            pltpu.SMEM((8, 128), jnp.int32),
            pltpu.SemaphoreType.DMA,
        ]
        + buffers(),
        compiler_params=pltpu.CompilerParams(vmem_limit_bytes=40 * MiB),
        cost_estimate=pl.CostEstimate(flops=4 << 30, bytes_accessed=4 << 20, transcendentals=0),
        name="edge",
    )(received)


def inner(bound, lists, received, edge_band, edge_rhs):
    vmem = pl.BlockSpec(memory_space=pltpu.VMEM)
    smem = pl.BlockSpec(memory_space=pltpu.SMEM)
    return pl.pallas_call(
        inner_kernel,
        out_shape=(
            jax.ShapeDtypeStruct((BLK_DEV, 2, 128, 128), F32),
            jax.ShapeDtypeStruct((BLK_DEV, 128), F32),
        ),
        in_specs=[smem, smem, vmem, vmem, vmem],
        out_specs=(vmem, vmem),
        scratch_shapes=buffers(),
        compiler_params=pltpu.CompilerParams(vmem_limit_bytes=40 * MiB),
        cost_estimate=pl.CostEstimate(flops=4 << 30, bytes_accessed=4 << 20, transcendentals=0),
        name="inner",
    )(bound, lists, received, edge_band, edge_rhs)


def on_device(spline_index, spline_frac, projection, forces, row_owner, row_offset):
    device_count = lax.axis_size(AXES)
    me = lax.axis_index(AXES).astype(jnp.int32).reshape(1)
    sent = pack(row_owner[:, 0], row_offset, me, spline_index, spline_frac, projection, forces, device_count)
    received = lax.all_to_all(sent, AXES, split_axis=0, concat_axis=0, tiled=True)
    edge_band, edge_rhs, spill, lists, bound = edge(received)
    route = [(i, (i + 1) % device_count) for i in range(device_count)]
    spill = lax.ppermute(spill, AXES, route)
    band, rhs = inner(bound, lists, received, edge_band, edge_rhs)
    band = band.at[0, 0].add(spill[0:128])
    rhs = rhs.at[0].add(spill[128])
    return band, rhs


def solution(mesh):
    in_specs = (
        P(AXES, None, None, None),
        P(AXES, None, None, None),
        P(AXES, None, None, None),
        P(AXES, None),
        P(AXES, None),
        P(AXES),
    )
    out_specs = (P(AXES, None, None, None), P(AXES, None))
    return jax.shard_map(
        on_device, mesh=mesh, in_specs=in_specs, out_specs=out_specs, check_vma=False
    )
```

time: 144 us -> 109 us (0.76)
  blocking collectives: 68.1 us -> 56 us
  starting transfers between devices: 11.6 us -> 1.01 us
  Pallas kernels: 48.7 us -> 41.4 us
  other arithmetic: 6.24 us -> 2.17 us
    all_gather x1 -> x0, blocking collectives: 68.1 us -> none  [on_device(): meta = lax.all_gather(jnp.stack([owners, row_offset]), AXES)]
    all_to_all x0 -> x1, blocking collectives: none -> 56 us  [on_device(): lax.all_to_all(sent, AXES, split_axis=0, concat_axis=0, tiled=True)]
    all_to_all x1 -> x0, starting transfers between devices: 11.5 us -> none  [on_device(): lax.all_to_all(sent, AXES, split_axis=0, concat_axis=0, tiled=True)]
    pallas_call x1, Pallas kernels: 21.5 us -> 16.8 us  [edge(): pl.pallas_call(edge_kernel, out_shape=(jax.ShapeDtypeStruct((2, 128, 128)...]
    pallas_call x1, Pallas kernels: 21.4 us -> 16.9 us  [inner(): pl.pallas_call(inner_kernel, out_shape=(jax.ShapeDtypeStruct((BLK_DEV, 2,...]
    another operation x2 -> x0, other arithmetic: 2.38 us -> none  [the longest x1 1.37 us: work_list(): jnp.stack([jnp.sum((slot_offset == BLK_DEV - 1).astype(jnp.int32)), jnp.s...]
    pallas_call x1, Pallas kernels: 5.79 us -> 7.77 us  [pack(): pl.pallas_call(pack_kernel, out_shape=jax.ShapeDtypeStruct((device_count,...]
    unnamed x16 -> x12, local copies, waits for them, and re-layouts: 5.82 us -> 5.45 us
  transfers between devices with their start and end apart: 2 -> 1, of which waited for: 0 -> 0; matrix products, arithmetic and copies ran while one was open for 4% -> 0% of each run, Pallas kernels for 15% -> 16%
where the time goes in v2:
time: 109 us; the launch traced here: 108 us
  blocking collectives  56 us (51%)
  Pallas kernels  41.4 us (38%)
  local copies, waits for them, and re-layouts  6.74 us (6%)
  other arithmetic  2.17 us (2%)
    all_to_all x1, blocking collectives, on_device(): lax.all_to_all(sent, AXES, split_axis=0, concat_axis=0, tiled=True)  56 us
    pallas_call x1, Pallas kernels, inner(): pl.pallas_call(inner_kernel, out_shape=(jax.ShapeDtypeStruct((BLK_DEV, 2,...  16.9 us
    pallas_call x1, Pallas kernels, edge(): pl.pallas_call(edge_kernel, out_shape=(jax.ShapeDtypeStruct((2, 128, 128)...  16.8 us
    pallas_call x1, Pallas kernels, pack(): pl.pallas_call(pack_kernel, out_shape=jax.ShapeDtypeStruct((device_count,...  7.77 us
    unnamed x12, local copies, waits for them, and re-layouts  5.45 us
  transfers between devices with their start and end apart: 1, of which 0 were waited for; matrix products, arithmetic and copies ran while one was open for 0% of the time, Pallas kernels for 16%

profile of v2, /device:TPU:1, one launch (start us, length us, event | category | flops | bytes accessed | tf_op | source)
XLA Modules:
  0.0 108.1 jit_solution(12318899191304585378)
XLA Ops:
  0.6 0.0 copy-start
  0.6 1.2 %copy-done = s32[128,2,4,256]{3,2,1,0:T(4,128)S(1)} copy-done((s32[128,2,4,256]{3,2,1,0:T(4,128)S(1)}, s32[128,2,4,256]{3,2,1,0:T(4,128)}, u32[]{:S(2)}) %copy-start) | copy-done | bytes 1048600
  1.9 0.0 copy-start.1
  1.9 1.0 copy-done.1
  2.9 0.0 copy-start.2
  2.9 1.0 copy-done.2
  3.9 0.0 copy-start.3
  4.0 0.8 copy-done.3
  4.8 0.0 copy-start.4
  4.8 0.7 copy-done.4
  5.4 0.0 copy-start.5
  5.4 0.7 copy-done.5
  6.1 7.8 %pack.1 = bf16[128,13,8,128]{3,2,1,0:T(8,128)(2,1)S(1)} custom-call(s32[128]{0:T(128)S(1)} %bitcast.8, s32[128]{0:T(128)S(1)} %copy-done.5, s32[1]{0:T(128)} %bitcast.1.me_ref, s32[128,2,4,256]{3,2,1,0:T(4,128)S(1)} %copy-done, bf16[128,2,4,256]{3,2,1,0:T(4,128)(2,1)S(1)} %copy-done.1, bf16[128,2,4,256]{3,2,1,0:T(4,128)(2,1)S(1)} %copy-done.2, ...), custom_call_target="tpu_custom_call" | custom-call | tf_op jit(solution)/shard_map/pack/pallas_call | solution.py:79
  13.9 56.0 %all_to_all.5.recv_ref = bf16[128,13,8,128]{3,2,1,0:T(8,128)(2,1)S(1)} all-to-all(bf16[128,13,8,128]{3,2,1,0:T(8,128)(2,1)S(1)} %pack.1), channel_id=1, replica_groups=mesh['frame'=4,'panel'=32] {'frame','panel'}, dimensions={0} | all-to-all | bytes 6815744 | tf_op jit(solution)/shard_map/all_to_all | solution.py:300
  69.9 16.8 %edge.1 = (f32[2,128,128]{2,1,0:T(8,128)S(1)}, f32[8,128]{1,0:T(8,128)S(1)}, f32[136,128]{1,0:T(8,128)S(1)}, s32[3,257]{1,0:T(4,128)S(1)}, s32[1]{0:T(128)}) custom-call(bf16[128,13,8,128]{3,2,1,0:T(8,128)(2,1)S(1)} %all_to_all.5.recv_ref), custom_call_target="tpu_custom_call" | custom-call | flops 4294967296 | bytes 4194304 | tf_op jit(solution)/shard_map/edge/pallas_call | solution.py:254
  86.7 1.0 collective-permute-start
  87.7 16.9 %inner.1 = (f32[22,2,128,128]{3,2,1,0:T(8,128)}, f32[22,128]{1,0:T(8,128)}) custom-call(s32[1]{0:T(128)} %get-tuple-element.33.bound_ref, s32[3,257]{1,0:T(4,128)S(1)} %get-tuple-element.34.list_ref, bf16[128,13,8,128]{3,2,1,0:T(8,128)(2,1)S(1)} %all_to_all.5.recv_ref, f32[2,128,128]{2,1,0:T(8,128)S(1)} %get-tuple-element.35.edge_band_ref, ...), custom_call_target="tpu_custom_call" | custom-call | flops 4294967296 | bytes 4194304 | tf_op jit(solution)/shard_map/inner/pallas_call | solution.py:281
  104.6 0.0 collective-permute-done
  104.6 0.7 slice_add_fusion
  105.3 1.3 %scatter-add.9 = f32[22,128]{1,0:T(8,128)} dynamic-update-slice(f32[22,128]{1,0:T(8,128)} %get-tuple-element.39, f32[1,128]{1,0:T(1,128)S(1)} %slice_add_fusion, s32[]{:T(128)} %constant.67.clone.1, s32[]{:T(128)} %constant.67.clone.1) | dynamic-update-slice | bytes 1028 | tf_op jit(solution)/shard_map/scatter-add | solution.py:306
  106.6 1.5 %fusion.1 = f32[22,2,128,128]{3,2,1,0:T(8,128)} fusion(f32[22,2,128,128]{3,2,1,0:T(8,128)} %get-tuple-element.37, f32[136,128]{1,0:T(8,128)S(1)} %collective-permute-done), kind=kLoop, calls=%fused_computation.2 | loop fusion | flops 16384 | bytes 196608 | tf_op jit(solution)/shard_map/scatter-add | solution.py:305
Async XLA Ops:
  0.6 1.2 %copy-start = (s32[128,2,4,256]{3,2,1,0:T(4,128)S(1)}, s32[128,2,4,256]{3,2,1,0:T(4,128)}, u32[]{:S(2)}) copy-start(s32[128,2,4,256]{3,2,1,0:T(4,128)} %index_hbm.1) | copy-start | bytes 3145732
  1.9 1.0 copy-start.1
  2.9 1.0 copy-start.2
  3.9 0.8 copy-start.3
  4.8 0.7 copy-start.4
  5.4 0.7 copy-start.5
  86.7 17.9 %collective-permute-start = (f32[136,128]{1,0:T(8,128)S(1)}, f32[136,128]{1,0:T(8,128)S(1)}, u32[]{:S(2)}, u32[]{:S(2)}) collective-permute-start(f32[136,128]{1,0:T(8,128)S(1)} %get-tuple-element.38), channel_id=1, source_target_pairs={{0,1},{1,2},{2,3},{3,4},{4,5},{5,6},{6,7},{7,8},{8,9},{9,10},{10,1... | collective-permute-start | bytes 208904 | tf_op jit(solution)/shard_map/ppermute | solution.py:303

commit v3 on v2

v3 whole, which is shorter than its diff:
```python
import jax
import jax.numpy as jnp
from jax import lax
from jax.experimental import pallas as pl
from jax.experimental.pallas import tpu as pltpu
from jax.sharding import PartitionSpec as P

CO = 128
BLK_DEV = 22
CAP = 2
AXES = ("frame", "panel")
BF16 = jnp.bfloat16
F32 = jnp.float32
CHUNKS = 8
MiB = 1 << 20


def pack_kernel(
    owner_ref, offset_ref, me_ref, index_hbm, frac_hbm, proj_hbm, force_hbm, out_hbm,
    count_ref, index_ref, frac_ref, proj_ref, force_ref, force_f32, tile_ref, tail_f32, tail_ref,
    in_sems, force_sem, out_sem, tail_sem,
):
    device_count = out_hbm.shape[0]
    tiles = owner_ref.shape[0]
    step = tiles // CHUNKS
    arrays = ((index_hbm, index_ref), (frac_hbm, frac_ref), (proj_hbm, proj_ref))

    def fetch(a, c):
        part = pl.ds(c * step, step)
        return pltpu.make_async_copy(arrays[a][0].at[part], arrays[a][1].at[part], in_sems.at[a, c])

    force_copy = pltpu.make_async_copy(force_hbm, force_ref, force_sem)
    force_copy.start()
    for c in range(CHUNKS):
        for a in range(3):
            fetch(a, c).start()

    @pl.loop(0, device_count, unroll=8)
    def _(d):
        count_ref[d] = 0

    tail_f32[...] = jnp.zeros_like(tail_f32)
    here = lax.broadcasted_iota(jnp.int32, (1, 128), 1) == me_ref[0]
    force_copy.wait()
    force_f32[...] = force_ref[...].astype(F32)

    for c in range(CHUNKS):
        for a in range(3):
            fetch(a, c).wait()

        @pl.loop(c * step, (c + 1) * step, unroll=2)
        def _(t):
            owner = owner_ref[t]
            place = count_ref[owner]
            count_ref[owner] = place + 1
            for a in range(3):
                ref = arrays[a][1]
                for g in range(2):
                    low = ref[t, 0, :, g * 128 : g * 128 + 128].astype(F32)
                    high = ref[t, 1, :, g * 128 : g * 128 + 128].astype(F32)
                    tile_ref[t, a * 2 + g] = jnp.concatenate([low, high], axis=0).astype(BF16)
            pltpu.make_async_copy(tile_ref.at[t], out_hbm.at[owner, pl.ds(place * 6, 6)], out_sem).start()
            row = force_f32[pl.ds(t, 1), :]
            for g in range(2):
                tail_f32[owner, pl.ds(place * 2 + g, 1), :] = row[:, g * 128 : g * 128 + 128]
            tail_f32[owner, pl.ds(4 + place, 1), :] = jnp.where(here, (offset_ref[t] + 1).astype(F32), 0.0)

    tail_ref[...] = tail_f32[...].astype(BF16)
    tail_copy = pltpu.make_async_copy(tail_ref, out_hbm.at[:, 12], tail_sem)
    tail_copy.start()
    tail_copy.wait()
    pltpu.make_async_copy(tile_ref, tile_ref, out_sem).wait()


def pack(owners, offsets, me, spline_index, spline_frac, projection, forces, device_count):
    hbm = pl.BlockSpec(memory_space=pltpu.HBM)
    smem = pl.BlockSpec(memory_space=pltpu.SMEM)
    tiles = owners.shape[0]
    return pl.pallas_call(
        pack_kernel,
        out_shape=jax.ShapeDtypeStruct((device_count, 13, 8, 128), BF16),
        in_specs=[smem, smem, smem, hbm, hbm, hbm, hbm],
        out_specs=hbm,
        scratch_shapes=[
            pltpu.SMEM((device_count,), jnp.int32),
            pltpu.VMEM(spline_index.shape, spline_index.dtype),
            pltpu.VMEM(spline_frac.shape, BF16),
            pltpu.VMEM(projection.shape, BF16),
            pltpu.VMEM(forces.shape, BF16),
            pltpu.VMEM(forces.shape, F32),
            pltpu.VMEM((tiles, 6, 8, 128), BF16),
            pltpu.VMEM((device_count, 8, 128), F32),
            pltpu.VMEM((device_count, 8, 128), BF16),
            pltpu.SemaphoreType.DMA((3, CHUNKS)),
            pltpu.SemaphoreType.DMA,
            pltpu.SemaphoreType.DMA,
            pltpu.SemaphoreType.DMA,
        ],
        compiler_params=pltpu.CompilerParams(vmem_limit_bytes=60 * MiB),
        name="pack",
    )(owners, offsets, me, spline_index, spline_frac, projection, forces)


def spline_rows(recv_ref, source, place, scale, bufs):
    base_buf, window_buf = bufs[0:2]
    pieces = [[], [], [], []]
    lows = []
    for g in range(2):
        index = recv_ref[source, place * 6 + g].astype(F32)
        t = recv_ref[source, place * 6 + 2 + g].astype(F32)
        q = recv_ref[source, place * 6 + 4 + g].astype(F32) * scale
        base_buf[g] = index * (1.0 / 16.0)
        lows.append((index.astype(jnp.int32) & 15).astype(F32))
        u = 1.0 - t
        t2 = t * t
        t3 = t2 * t
        pieces[0].append(q * (u * u * u))
        pieces[1].append(q * (3.0 * t3 - 6.0 * t2 + 4.0))
        pieces[2].append(q * (3.0 * (t + t2 - t3) + 1.0))
        pieces[3].append(q * t3)
    low = jnp.concatenate(lows, axis=0).astype(BF16)
    pieces = [jnp.concatenate(p, axis=0).astype(BF16) for p in pieces]
    starts = [low == k for k in range(16)]
    zero = jnp.zeros((16, 128), BF16)
    for k in range(16):
        value = zero
        for m in range(4):
            value = jnp.where(starts[(k - m) % 16], pieces[m], value)
        value = value.astype(F32)
        for g in range(2):
            window_buf[g, pl.ds(k, 8, stride=24), :] = value[g * 8 : g * 8 + 8]


def build_design(bufs):
    base_buf, window_buf, design_buf = bufs[0:3]
    shift = (lax.broadcasted_iota(jnp.int32, (16, 128), 0).astype(F32) * (1.0 / 16.0) - 7.5 / 16.0).astype(BF16)
    zero = jnp.zeros((16, 128), BF16)
    for s in range(2):
        for g in range(2):
            blocks = [None] * 8
            for n in range(4):
                row = s * 4 + n
                base = base_buf[g, pl.ds(row, 8, stride=0), :]
                base = jnp.concatenate([base, base], axis=0).astype(BF16)
                home = (base - shift) + 128
                window = window_buf[g, row * 24 : row * 24 + 16, :].astype(BF16)
                for b in range(8):
                    piece = jnp.where(home == 128 + b, window, zero)
                    blocks[b] = piece if n == 0 else blocks[b] + piece
            for b in range(8):
                design_buf[g, s * 128 + b * 16 : s * 128 + b * 16 + 16, :] = blocks[b]


def force_rows(recv_ref, source, place, bufs):
    design_buf, force_buf = bufs[2:4]
    force_buf[...] = recv_ref[source, 12].astype(F32)
    first = lax.broadcasted_iota(jnp.int32, (16, 128), 0) == 0
    for g in range(2):
        row = force_buf[pl.ds(place * 2 + g, 8, stride=0), :]
        row = jnp.concatenate([row, row], axis=0)
        design_buf[g, 256:272, :] = jnp.where(first, row, 0.0).astype(BF16)


def build_tile(recv_ref, word, scale, bufs):
    source = (word >> 1) & 127
    place = word & 1
    spline_rows(recv_ref, source, place, scale, bufs)
    force_rows(recv_ref, source, place, bufs)
    build_design(bufs)


def products(bufs):
    design_buf = bufs[2]
    both = jnp.concatenate([design_buf[0], design_buf[1]], axis=1)
    return lax.dot_general(both, both[0:256], (((1,), (1,)), ((), ())), preferred_element_type=F32)


def sweep(count, word_at, recv_ref, add, bufs):
    bufs[2][...] = jnp.zeros_like(bufs[2])

    def step(i, carry):
        out = products(bufs)
        build_tile(recv_ref, word_at(i), 1.0 / 6.0, bufs)
        add(word_at(jnp.maximum(i - 1, 0)), out)
        return carry

    lax.fori_loop(0, count, step, 0)

    @pl.when(count > 0)
    def _():
        add(word_at(count - 1), products(bufs))


def edge_kernel(
    recv_ref, band_ref, rhs_ref, spill_ref, inner_list, bound_ref, meta_i32, first_mark, second_mark, edge_list,
    meta_sems, *bufs,
):
    devices = recv_ref.shape[0]
    totals = [jnp.zeros((8, 128), F32)] * 4
    for d in range(devices):
        totals[d % 4] = totals[d % 4] + recv_ref[d, 12].astype(F32)
    meta_i32[...] = (totals[0] + totals[1] + totals[2] + totals[3]).astype(jnp.int32)
    marks = (first_mark, second_mark)
    copies = [pltpu.make_async_copy(meta_i32.at[4 + q], marks[q], meta_sems.at[q]) for q in range(CAP)]
    for copy in copies:
        copy.start()
    band_ref[...] = jnp.zeros_like(band_ref)
    rhs_ref[...] = jnp.zeros_like(rhs_ref)
    spill_ref[...] = jnp.zeros_like(spill_ref)
    for copy in copies:
        copy.wait()

    def scan(d, counts):
        edges, others = counts
        for q in range(CAP):
            mark = marks[q][d]
            word = (mark << 8) + (d * CAP + q)
            at_edge = (mark == BLK_DEV).astype(jnp.int32)
            filled = jnp.minimum(mark, 1)
            edge_list[edges] = word
            inner_list[others] = word
            edges = edges + at_edge
            others = others + (filled - at_edge)
        return edges, others

    edges, others = lax.fori_loop(0, devices, scan, (0, 0), unroll=8)
    bound_ref[0] = others

    def add(word, out):
        band_ref[0] += out[0:128, 0:128]
        band_ref[1] += out[0:128, 128:256]
        spill_ref[0:128, :] += out[128:256, 128:256]
        rhs_ref[...] += out[256:264, 0:128]
        spill_ref[128:136, :] += out[256:264, 128:256]

    sweep(edges, lambda i: edge_list[i], recv_ref, add, bufs)


def inner_kernel(bound_ref, list_ref, recv_ref, edge_band_ref, edge_rhs_ref, band_ref, rhs_ref, *bufs):
    last = band_ref.shape[0] - 1
    band_ref[0:last] = jnp.zeros((last, 2, 128, 128), F32)
    band_ref[last] = edge_band_ref[...]
    rhs_ref[...] = jnp.zeros_like(rhs_ref)
    rhs_ref[last:last + 1] = edge_rhs_ref[0:1, :]

    def add(word, out):
        at = (word >> 8) - 1
        band_ref[at, 0] += out[0:128, 0:128]
        band_ref[at, 1] += out[0:128, 128:256]
        band_ref[at + 1, 0] += out[128:256, 128:256]
        rhs_ref[pl.ds(at, 1), :] += out[256:257, 0:128]
        rhs_ref[pl.ds(at + 1, 1), :] += out[256:257, 128:256]

    sweep(bound_ref[0], lambda i: list_ref[i], recv_ref, add, bufs)


def finish_kernel(band_ref, rhs_ref, spill_ref, band_hbm, rhs_hbm, first_band, first_rhs, sems):
    rest = pltpu.make_async_copy(band_ref.at[1:], band_hbm.at[1:], sems.at[0])
    lag = pltpu.make_async_copy(band_ref.at[0, 1], band_hbm.at[0, 1], sems.at[1])
    rest.start()
    lag.start()
    first_band[...] = band_ref[0, 0] + spill_ref[0:128, :]
    first_rhs[...] = rhs_ref[...]
    first_rhs[0:1, :] = rhs_ref[0:1, :] + spill_ref[128:129, :]
    diagonal = pltpu.make_async_copy(first_band, band_hbm.at[0, 0], sems.at[2])
    right = pltpu.make_async_copy(first_rhs, rhs_hbm, sems.at[3])
    diagonal.start()
    right.start()
    right.wait()
    diagonal.wait()
    lag.wait()
    rest.wait()


def buffers():
    return [
        pltpu.VMEM((2, 8, 128), F32),
        pltpu.VMEM((2, 192, 128), F32),
        pltpu.VMEM((2, 272, 128), BF16),
        pltpu.VMEM((8, 128), F32),
    ]


VMEM = pl.BlockSpec(memory_space=pltpu.VMEM)
SMEM = pl.BlockSpec(memory_space=pltpu.SMEM)
HBM = pl.BlockSpec(memory_space=pltpu.HBM)
SWEEP_COST = pl.CostEstimate(flops=4 << 30, bytes_accessed=4 << 20, transcendentals=0)


def edge(received):
    devices = received.shape[0]
    return pl.pallas_call(
        edge_kernel,
        out_shape=(
            jax.ShapeDtypeStruct((2, 128, 128), F32),
            jax.ShapeDtypeStruct((8, 128), F32),
            jax.ShapeDtypeStruct((136, 128), F32),
            jax.ShapeDtypeStruct((devices * CAP + 8,), jnp.int32),
            jax.ShapeDtypeStruct((1,), jnp.int32),
        ),
        in_specs=[VMEM],
        out_specs=(VMEM, VMEM, VMEM, SMEM, SMEM),
        scratch_shapes=[
            pltpu.VMEM((8, 128), jnp.int32),
            pltpu.SMEM((128,), jnp.int32),
            pltpu.SMEM((128,), jnp.int32),
            pltpu.SMEM((devices * CAP + 8,), jnp.int32),
            pltpu.SemaphoreType.DMA((CAP,)),
        ]
        + buffers(),
        compiler_params=pltpu.CompilerParams(vmem_limit_bytes=40 * MiB),
        cost_estimate=SWEEP_COST,
        name="edge",
    )(received)


def inner(bound, lists, received, edge_band, edge_rhs):
    return pl.pallas_call(
        inner_kernel,
        out_shape=(
            jax.ShapeDtypeStruct((BLK_DEV, 2, 128, 128), F32),
            jax.ShapeDtypeStruct((BLK_DEV, 128), F32),
        ),
        in_specs=[SMEM, SMEM, VMEM, VMEM, VMEM],
        out_specs=(VMEM, VMEM),
        scratch_shapes=buffers(),
        compiler_params=pltpu.CompilerParams(vmem_limit_bytes=40 * MiB),
        cost_estimate=SWEEP_COST,
        name="inner",
    )(bound, lists, received, edge_band, edge_rhs)


def finish(band, rhs, spill):
    return pl.pallas_call(
        finish_kernel,
        out_shape=(jax.ShapeDtypeStruct(band.shape, F32), jax.ShapeDtypeStruct(rhs.shape, F32)),
        in_specs=[VMEM, VMEM, VMEM],
        out_specs=(HBM, HBM),
        scratch_shapes=[
            pltpu.VMEM((128, 128), F32),
            pltpu.VMEM(rhs.shape, F32),
            pltpu.SemaphoreType.DMA((4,)),
        ],
        compiler_params=pltpu.CompilerParams(vmem_limit_bytes=16 * MiB),
        name="finish",
    )(band, rhs, spill)


def on_device(spline_index, spline_frac, projection, forces, row_owner, row_offset):
    device_count = lax.axis_size(AXES)
    me = lax.axis_index(AXES).astype(jnp.int32).reshape(1)
    sent = pack(row_owner[:, 0], row_offset, me, spline_index, spline_frac, projection, forces, device_count)
    received = lax.all_to_all(sent, AXES, split_axis=0, concat_axis=0, tiled=True)
    edge_band, edge_rhs, spill, lists, bound = edge(received)
    route = [(i, (i + 1) % device_count) for i in range(device_count)]
    spill = lax.ppermute(spill, AXES, route)
    band, rhs = inner(bound, lists, received, edge_band, edge_rhs)
    return finish(band, rhs, spill)


def solution(mesh):
    in_specs = (
        P(AXES, None, None, None),
        P(AXES, None, None, None),
        P(AXES, None, None, None),
        P(AXES, None),
        P(AXES, None),
        P(AXES),
    )
    out_specs = (P(AXES, None, None, None), P(AXES, None))
    return jax.shard_map(
        on_device, mesh=mesh, in_specs=in_specs, out_specs=out_specs, check_vma=False
    )
```

time: 109 us -> 101 us (0.927)
  local copies, waits for them, and re-layouts: 6.74 us -> 0 us
  other arithmetic: 2.17 us -> 0 us
  Pallas kernels: 41.4 us -> 42.8 us
    unnamed x12 -> x0, local copies, waits for them, and re-layouts: 5.45 us -> none
    pallas_call x1, Pallas kernels: 7.77 us -> 4.78 us  [pack(): pl.pallas_call(pack_kernel, out_shape=jax.ShapeDtypeStruct((device_count,...]
    pallas_call x1, Pallas kernels: 16.8 us -> 19.1 us  [edge(): pl.pallas_call(edge_kernel, out_shape=(jax.ShapeDtypeStruct((2, 128, 128)...]
    pallas_call x0 -> x1, Pallas kernels: none -> 1.6 us  [finish(): pl.pallas_call(finish_kernel, out_shape=(jax.ShapeDtypeStruct(band.shape,...]
    scatter-add x1 -> x0, other arithmetic: 1.48 us -> none  [on_device(): band = band.at[0, 0].add(spill[0:128])]
    scatter-add x1 -> x0, local copies, waits for them, and re-layouts: 1.29 us -> none  [on_device(): rhs = rhs.at[0].add(spill[128])]
  transfers between devices with their start and end apart: 1 -> 1, of which waited for: 0 -> 0; matrix products, arithmetic and copies ran while one was open for 0% -> 0% of each run, Pallas kernels for 16% -> 17%
where the time goes in v3:
time: 101 us
  blocking collectives  56.3 us (56%)
  Pallas kernels  42.8 us (42%)
  starting transfers between devices  1.02 us (1%)
    all_to_all x1, blocking collectives, on_device(): lax.all_to_all(sent, AXES, split_axis=0, concat_axis=0, tiled=True)  56.3 us
    pallas_call x1, Pallas kernels, edge(): pl.pallas_call(edge_kernel, out_shape=(jax.ShapeDtypeStruct((2, 128, 128)...  19.1 us
    pallas_call x1, Pallas kernels, inner(): pl.pallas_call(inner_kernel, out_shape=(jax.ShapeDtypeStruct((BLK_DEV, 2,...  17.3 us
    pallas_call x1, Pallas kernels, pack(): pl.pallas_call(pack_kernel, out_shape=jax.ShapeDtypeStruct((device_count,...  4.78 us
  transfers between devices with their start and end apart: 1, of which 0 were waited for; matrix products, arithmetic and copies ran while one was open for 0% of the time, Pallas kernels for 17%

profile of v3, /device:TPU:1, one launch (start us, length us, event | category | flops | bytes accessed | tf_op | source)
XLA Modules:
  0.0 100.7 jit_solution(10554555450328149711)
XLA Ops:
  0.6 4.8 %pack.1 = bf16[128,13,8,128]{3,2,1,0:T(8,128)(2,1)} custom-call(s32[128]{0:T(128)} %bitcast.2, s32[128]{0:T(128)} %offset_ref.1, s32[1]{0:T(128)} %bitcast.1.me_ref, s32[128,2,4,256]{3,2,1,0:T(4,128)} %index_hbm.1, bf16[128,2,4,256]{3,2,1,0:T(4,128)(2,1)} %frac_hbm.1, bf16[128,2,4,256]{3,2,1,0:T(4,128)(2,1)} %proj_hbm.1, bf16[128,256]{1,0:T(8,128)(2,1)} %force_hbm.1), custom_call_target="tpu_custom_call" | custom-call | tf_op jit(solution)/shard_map/pack/pallas_call | solution.py:79
  5.4 56.3 %all_to_all.5.recv_ref = bf16[128,13,8,128]{3,2,1,0:T(8,128)(2,1)S(1)} all-to-all(bf16[128,13,8,128]{3,2,1,0:T(8,128)(2,1)} %pack.1), channel_id=1, replica_groups=mesh['frame'=4,'panel'=32] {'frame','panel'}, dimensions={0} | all-to-all | bytes 6815744 | tf_op jit(solution)/shard_map/all_to_all | solution.py:353
  61.7 19.1 %edge.1 = (f32[2,128,128]{2,1,0:T(8,128)S(1)}, f32[8,128]{1,0:T(8,128)S(1)}, f32[136,128]{1,0:T(8,128)S(1)}, s32[264]{0:T(512)S(1)}, s32[1]{0:T(128)}) custom-call(bf16[128,13,8,128]{3,2,1,0:T(8,128)(2,1)S(1)} %all_to_all.5.recv_ref), custom_call_target="tpu_custom_call" | custom-call | flops 4294967296 | bytes 4194304 | tf_op jit(solution)/shard_map/edge/pallas_call | solution.py:292
  80.8 1.0 %collective-permute-start = (f32[136,128]{1,0:T(8,128)S(1)}, f32[136,128]{1,0:T(8,128)S(1)}, u32[]{:S(2)}, u32[]{:S(2)}) collective-permute-start(f32[136,128]{1,0:T(8,128)S(1)} %get-tuple-element.15), channel_id=1, source_target_pairs={{0,1},{1,2},{2,3},{3,4},{4,5},{5,6},{6,7},{7,8},{8,9},{9,10},{10,1... | collective-permute-start | bytes 208904 | tf_op jit(solution)/shard_map/ppermute | solution.py:356
  81.8 17.3 %inner.1 = (f32[22,2,128,128]{3,2,1,0:T(8,128)S(1)}, f32[22,128]{1,0:T(8,128)S(1)}) custom-call(s32[1]{0:T(128)} %get-tuple-element.9.bound_ref, s32[264]{0:T(512)S(1)} %get-tuple-element.10.list_ref, bf16[128,13,8,128]{3,2,1,0:T(8,128)(2,1)S(1)} %all_to_all.5.recv_ref, f32[2,128,128]{2,1,0:T(8,128)S(1)} %get-tuple-element.11.edge_band_ref, ...), custom_call_target="tpu_custom_call" | custom-call | flops 4294967296 | bytes 4194304 | tf_op jit(solution)/shard_map/inner/pallas_call | solution.py:318
  99.1 0.0 collective-permute-done.spill_ref
  99.1 1.6 %finish.1 = (f32[22,2,128,128]{3,2,1,0:T(8,128)}, f32[22,128]{1,0:T(8,128)}) custom-call(f32[22,2,128,128]{3,2,1,0:T(8,128)S(1)} %get-tuple-element.13.band_ref, f32[22,128]{1,0:T(8,128)S(1)} %get-tuple-element.14.rhs_ref, f32[136,128]{1,0:T(8,128)S(1)} %collective-permute-done.spill_ref), custom_call_target="tpu_custom_call" | custom-call | tf_op jit(solution)/shard_map/finish/pallas_call | solution.py:334
Async XLA Ops:
  80.8 18.4 %collective-permute-start = (f32[136,128]{1,0:T(8,128)S(1)}, f32[136,128]{1,0:T(8,128)S(1)}, u32[]{:S(2)}, u32[]{:S(2)}) collective-permute-start(f32[136,128]{1,0:T(8,128)S(1)} %get-tuple-element.15), channel_id=1, source_target_pairs={{0,1},{1,2},{2,3},{3,4},{4,5},{5,6},{6,7},{7,8},{8,9},{9,10},{10,1... | collective-permute-start | bytes 208904 | tf_op jit(solution)/shard_map/ppermute | solution.py:356

commit v4 on v3

--- a/solution.py
+++ b/solution.py
@@ -12,6 +12,7 @@
 BF16 = jnp.bfloat16
 F32 = jnp.float32
 CHUNKS = 8
+GROUP = 4
 MiB = 1 << 20
 
 
@@ -176,19 +177,30 @@
 
 
 def sweep(count, word_at, recv_ref, add, bufs):
-    bufs[2][...] = jnp.zeros_like(bufs[2])
-
-    def step(i, carry):
-        out = products(bufs)
-        build_tile(recv_ref, word_at(i), 1.0 / 6.0, bufs)
-        add(word_at(jnp.maximum(i - 1, 0)), out)
+    sets = [bufs[u * 4 : u * 4 + 4] for u in range(GROUP)]
+    for group in sets:
+        group[2][...] = jnp.zeros_like(group[2])
+
+    def clamped(i):
+        return word_at(jnp.clip(i, 0, count - 1))
+
+    def step(j, carry):
+        first = j * GROUP
+        for u in range(GROUP):
+            out = products(sets[u])
+            i = first + u
+            scale = jnp.where(i < count, 1.0 / 6.0, 0.0).astype(F32)
+            build_tile(recv_ref, clamped(i), scale, sets[u])
+            add(clamped(i - GROUP), out)
         return carry
 
-    lax.fori_loop(0, count, step, 0)
+    turns = (count + GROUP - 1) // GROUP
+    lax.fori_loop(0, turns, step, 0)
 
     @pl.when(count > 0)
     def _():
-        add(word_at(count - 1), products(bufs))
+        for u in range(GROUP):
+            add(clamped((turns - 1) * GROUP + u), products(sets[u]))
 
 
 def edge_kernel(
@@ -278,7 +290,7 @@
         pltpu.VMEM((2, 192, 128), F32),
         pltpu.VMEM((2, 272, 128), BF16),
         pltpu.VMEM((8, 128), F32),
-    ]
+    ] * GROUP
 
 
 VMEM = pl.BlockSpec(memory_space=pltpu.VMEM)

time: 101 us -> 86.3 us (0.85)
  Pallas kernels: 42.8 us -> 27.8 us
    pallas_call x1, Pallas kernels: 19.1 us -> 11.1 us  [edge(): pl.pallas_call(edge_kernel, out_shape=(jax.ShapeDtypeStruct((2, 128, 128)...]
    pallas_call x1, Pallas kernels: 17.3 us -> 10.3 us  [inner(): pl.pallas_call(inner_kernel, out_shape=(jax.ShapeDtypeStruct((BLK_DEV, 2,...]
  transfers between devices with their start and end apart: 1 -> 1, of which waited for: 0 -> 0; matrix products, arithmetic and copies ran while one was open for 0% -> 0% of each run, Pallas kernels for 17% -> 12%
where the time goes in v4:
time: 86.3 us; the launch traced here: 85.7 us
  blocking collectives  56.3 us (65%)
  Pallas kernels  27.8 us (32%)
  starting transfers between devices  1.02 us (1%)
    all_to_all x1, blocking collectives, on_device(): lax.all_to_all(sent, AXES, split_axis=0, concat_axis=0, tiled=True)  56.3 us
    pallas_call x1, Pallas kernels, edge(): pl.pallas_call(edge_kernel, out_shape=(jax.ShapeDtypeStruct((2, 128, 128)...  11.1 us
    pallas_call x1, Pallas kernels, inner(): pl.pallas_call(inner_kernel, out_shape=(jax.ShapeDtypeStruct((BLK_DEV, 2,...  10.3 us
    pallas_call x1, Pallas kernels, pack(): pl.pallas_call(pack_kernel, out_shape=jax.ShapeDtypeStruct((device_count,...  4.78 us
  transfers between devices with their start and end apart: 1, of which 0 were waited for; matrix products, arithmetic and copies ran while one was open for 0% of the time, Pallas kernels for 12%

profile of v4, /device:TPU:1, one launch (start us, length us, event | category | flops | bytes accessed | tf_op | source)
XLA Modules:
  0.0 85.7 jit_solution(4046026163911417730)
XLA Ops:
  0.6 4.8 %pack.1 = bf16[128,13,8,128]{3,2,1,0:T(8,128)(2,1)} custom-call(s32[128]{0:T(128)} %bitcast.2, s32[128]{0:T(128)} %offset_ref.1, s32[1]{0:T(128)} %bitcast.1.me_ref, s32[128,2,4,256]{3,2,1,0:T(4,128)} %index_hbm.1, bf16[128,2,4,256]{3,2,1,0:T(4,128)(2,1)} %frac_hbm.1, bf16[128,2,4,256]{3,2,1,0:T(4,128)(2,1)} %proj_hbm.1, bf16[128,256]{1,0:T(8,128)(2,1)} %force_hbm.1), custom_call_target="tpu_custom_call" | custom-call | tf_op jit(solution)/shard_map/pack/pallas_call | solution.py:80
  5.4 56.3 %all_to_all.5.recv_ref = bf16[128,13,8,128]{3,2,1,0:T(8,128)(2,1)S(1)} all-to-all(bf16[128,13,8,128]{3,2,1,0:T(8,128)(2,1)} %pack.1), channel_id=1, replica_groups=mesh['frame'=4,'panel'=32] {'frame','panel'}, dimensions={0} | all-to-all | bytes 6815744 | tf_op jit(solution)/shard_map/all_to_all | solution.py:365
  61.7 11.1 %edge.1 = (f32[2,128,128]{2,1,0:T(8,128)S(1)}, f32[8,128]{1,0:T(8,128)S(1)}, f32[136,128]{1,0:T(8,128)S(1)}, s32[264]{0:T(512)S(1)}, s32[1]{0:T(128)}) custom-call(bf16[128,13,8,128]{3,2,1,0:T(8,128)(2,1)S(1)} %all_to_all.5.recv_ref), custom_call_target="tpu_custom_call" | custom-call | flops 4294967296 | bytes 4194304 | tf_op jit(solution)/shard_map/edge/pallas_call | solution.py:304
  72.8 1.0 %collective-permute-start = (f32[136,128]{1,0:T(8,128)S(1)}, f32[136,128]{1,0:T(8,128)S(1)}, u32[]{:S(2)}, u32[]{:S(2)}) collective-permute-start(f32[136,128]{1,0:T(8,128)S(1)} %get-tuple-element.15), channel_id=1, source_target_pairs={{0,1},{1,2},{2,3},{3,4},{4,5},{5,6},{6,7},{7,8},{8,9},{9,10},{10,1... | collective-permute-start | bytes 208904 | tf_op jit(solution)/shard_map/ppermute | solution.py:368
  73.8 10.3 %inner.1 = (f32[22,2,128,128]{3,2,1,0:T(8,128)S(1)}, f32[22,128]{1,0:T(8,128)S(1)}) custom-call(s32[1]{0:T(128)} %get-tuple-element.9.bound_ref, s32[264]{0:T(512)S(1)} %get-tuple-element.10.list_ref, bf16[128,13,8,128]{3,2,1,0:T(8,128)(2,1)S(1)} %all_to_all.5.recv_ref, f32[2,128,128]{2,1,0:T(8,128)S(1)} %get-tuple-element.11.edge_band_ref, ...), custom_call_target="tpu_custom_call" | custom-call | flops 4294967296 | bytes 4194304 | tf_op jit(solution)/shard_map/inner/pallas_call | solution.py:330
  84.1 0.0 collective-permute-done.spill_ref
  84.1 1.6 %finish.1 = (f32[22,2,128,128]{3,2,1,0:T(8,128)}, f32[22,128]{1,0:T(8,128)}) custom-call(f32[22,2,128,128]{3,2,1,0:T(8,128)S(1)} %get-tuple-element.13.band_ref, f32[22,128]{1,0:T(8,128)S(1)} %get-tuple-element.14.rhs_ref, f32[136,128]{1,0:T(8,128)S(1)} %collective-permute-done.spill_ref), custom_call_target="tpu_custom_call" | custom-call | tf_op jit(solution)/shard_map/finish/pallas_call | solution.py:346
Async XLA Ops:
  72.8 11.4 %collective-permute-start = (f32[136,128]{1,0:T(8,128)S(1)}, f32[136,128]{1,0:T(8,128)S(1)}, u32[]{:S(2)}, u32[]{:S(2)}) collective-permute-start(f32[136,128]{1,0:T(8,128)S(1)} %get-tuple-element.15), channel_id=1, source_target_pairs={{0,1},{1,2},{2,3},{3,4},{4,5},{5,6},{6,7},{7,8},{8,9},{9,10},{10,1... | collective-permute-start | bytes 208904 | tf_op jit(solution)/shard_map/ppermute | solution.py:368

commit v5 on v4

--- a/solution.py
+++ b/solution.py
@@ -12,7 +12,7 @@
 BF16 = jnp.bfloat16
 F32 = jnp.float32
 CHUNKS = 8
-GROUP = 4
+GROUP = 8
 MiB = 1 << 20
 
 
@@ -110,8 +110,8 @@
         index = recv_ref[source, place * 6 + g].astype(F32)
         t = recv_ref[source, place * 6 + 2 + g].astype(F32)
         q = recv_ref[source, place * 6 + 4 + g].astype(F32) * scale
-        base_buf[g] = index * (1.0 / 16.0)
-        lows.append((index.astype(jnp.int32) & 15).astype(F32))
+        base_buf[g] = index * (1.0 / 8.0)
+        lows.append((index.astype(jnp.int32) & 7).astype(F32))
         u = 1.0 - t
         t2 = t * t
         t3 = t2 * t
@@ -121,45 +121,50 @@
         pieces[3].append(q * t3)
     low = jnp.concatenate(lows, axis=0).astype(BF16)
     pieces = [jnp.concatenate(p, axis=0).astype(BF16) for p in pieces]
-    starts = [low == k for k in range(16)]
+    starts = [low == k for k in range(8)]
     zero = jnp.zeros((16, 128), BF16)
-    for k in range(16):
+    for k in range(8):
         value = zero
         for m in range(4):
-            value = jnp.where(starts[(k - m) % 16], pieces[m], value)
+            value = jnp.where(starts[(k - m) % 8], pieces[m], value)
         value = value.astype(F32)
         for g in range(2):
-            window_buf[g, pl.ds(k, 8, stride=24), :] = value[g * 8 : g * 8 + 8]
+            window_buf[g, pl.ds(k, 8, stride=8), :] = value[g * 8 : g * 8 + 8]
 
 
 def build_design(bufs):
     base_buf, window_buf, design_buf = bufs[0:3]
-    shift = (lax.broadcasted_iota(jnp.int32, (16, 128), 0).astype(F32) * (1.0 / 16.0) - 7.5 / 16.0).astype(BF16)
+    k = (lax.broadcasted_iota(jnp.int32, (16, 128), 0) & 7).astype(F32)
+    shift = (k * (1.0 / 8.0) - 7.0 / 16.0).astype(BF16)
     zero = jnp.zeros((16, 128), BF16)
     for s in range(2):
-        for g in range(2):
-            blocks = [None] * 8
-            for n in range(4):
-                row = s * 4 + n
-                base = base_buf[g, pl.ds(row, 8, stride=0), :]
-                base = jnp.concatenate([base, base], axis=0).astype(BF16)
-                home = (base - shift) + 128
-                window = window_buf[g, row * 24 : row * 24 + 16, :].astype(BF16)
-                for b in range(8):
-                    piece = jnp.where(home == 128 + b, window, zero)
-                    blocks[b] = piece if n == 0 else blocks[b] + piece
-            for b in range(8):
-                design_buf[g, s * 128 + b * 16 : s * 128 + b * 16 + 16, :] = blocks[b]
+        blocks = [None] * 16
+        for n in range(4):
+            row = s * 4 + n
+            base = [base_buf[g, pl.ds(row, 8, stride=0), :] for g in range(2)]
+            base = jnp.concatenate(base, axis=0).astype(BF16)
+            home = (base - shift) + 128
+            window = [window_buf[g, row * 8 : row * 8 + 8, :] for g in range(2)]
+            window = jnp.concatenate(window, axis=0).astype(BF16)
+            for b in range(16):
+                piece = jnp.where(home == 128 + b, window, zero)
+                blocks[b] = piece if n == 0 else blocks[b] + piece
+        for b in range(16):
+            at = s * 128 + b * 8
+            design_buf[at : at + 8, 0:128] = blocks[b][0:8]
+            design_buf[at : at + 8, 128:256] = blocks[b][8:16]
 
 
 def force_rows(recv_ref, source, place, bufs):
     design_buf, force_buf = bufs[2:4]
     force_buf[...] = recv_ref[source, 12].astype(F32)
     first = lax.broadcasted_iota(jnp.int32, (16, 128), 0) == 0
+    rows = []
     for g in range(2):
         row = force_buf[pl.ds(place * 2 + g, 8, stride=0), :]
         row = jnp.concatenate([row, row], axis=0)
-        design_buf[g, 256:272, :] = jnp.where(first, row, 0.0).astype(BF16)
+        rows.append(jnp.where(first, row, 0.0).astype(BF16))
+    design_buf[256:272, :] = jnp.concatenate(rows, axis=1)
 
 
 def build_tile(recv_ref, word, scale, bufs):
@@ -172,8 +177,9 @@
 
 def products(bufs):
     design_buf = bufs[2]
-    both = jnp.concatenate([design_buf[0], design_buf[1]], axis=1)
-    return lax.dot_general(both, both[0:256], (((1,), (1,)), ((), ())), preferred_element_type=F32)
+    return lax.dot_general(
+        design_buf[...], design_buf[0:256, :], (((1,), (1,)), ((), ())), preferred_element_type=F32
+    )
 
 
 def sweep(count, word_at, recv_ref, add, bufs):
@@ -204,16 +210,34 @@
 
 
 def edge_kernel(
-    recv_ref, band_ref, rhs_ref, spill_ref, inner_list, bound_ref, meta_i32, first_mark, second_mark, edge_list,
-    meta_sems, *bufs,
+    recv_ref, band_ref, rhs_ref, spill_ref, list_ref, bound_ref, meta_i32, first_words, second_words, edge_count,
+    other_count, meta_sems, *bufs,
 ):
+    counts = (edge_count, other_count)
     devices = recv_ref.shape[0]
     totals = [jnp.zeros((8, 128), F32)] * 4
     for d in range(devices):
         totals[d % 4] = totals[d % 4] + recv_ref[d, 12].astype(F32)
-    meta_i32[...] = (totals[0] + totals[1] + totals[2] + totals[3]).astype(jnp.int32)
-    marks = (first_mark, second_mark)
-    copies = [pltpu.make_async_copy(meta_i32.at[4 + q], marks[q], meta_sems.at[q]) for q in range(CAP)]
+    mark = (totals[0] + totals[1] + totals[2] + totals[3])[4 : 4 + CAP]
+    at_edge = mark == BLK_DEV
+    other = (mark > 0) & (mark < BLK_DEV)
+    kinds = jnp.concatenate([at_edge.astype(F32), other.astype(F32), jnp.zeros((4, 128), F32)], axis=0)
+    ahead = lax.broadcasted_iota(jnp.int32, (128, 128), 0) < lax.broadcasted_iota(jnp.int32, (128, 128), 1)
+    rank = lax.dot_general(
+        kinds.astype(BF16), ahead.astype(F32).astype(BF16), (((1,), (0,)), ((), ())), preferred_element_type=F32
+    )
+    sums = jnp.sum(kinds, axis=1, keepdims=True)
+    rank_edge = jnp.concatenate([rank[0:1], rank[1:2] + sums[0:1]], axis=0)
+    rank_other = jnp.concatenate([rank[2:3], rank[3:4] + sums[2:3]], axis=0)
+    slots = devices * CAP
+    where_to = jnp.where(at_edge, rank_edge, jnp.where(other, slots - 1 - rank_other, slots)).astype(jnp.int32)
+    shape = (CAP, 128)
+    code = lax.broadcasted_iota(jnp.int32, shape, 1) * CAP + lax.broadcasted_iota(jnp.int32, shape, 0)
+    meta_i32[0:CAP] = where_to * 65536 + mark.astype(jnp.int32) * 256 + code
+    meta_i32[2:3] = jnp.broadcast_to(sums[0:1] + sums[1:2], (1, 128)).astype(jnp.int32)
+    meta_i32[3:4] = jnp.broadcast_to(sums[2:3] + sums[3:4], (1, 128)).astype(jnp.int32)
+    words = (first_words, second_words)
+    copies = [pltpu.make_async_copy(meta_i32.at[k], ref, meta_sems.at[k]) for k, ref in enumerate(words + tuple(counts))]
     for copy in copies:
         copy.start()
     band_ref[...] = jnp.zeros_like(band_ref)
@@ -222,21 +246,13 @@
     for copy in copies:
         copy.wait()
 
-    def scan(d, counts):
-        edges, others = counts
+    @pl.loop(0, devices, unroll=8)
+    def _(d):
         for q in range(CAP):
-            mark = marks[q][d]
-            word = (mark << 8) + (d * CAP + q)
-            at_edge = (mark == BLK_DEV).astype(jnp.int32)
-            filled = jnp.minimum(mark, 1)
-            edge_list[edges] = word
-            inner_list[others] = word
-            edges = edges + at_edge
-            others = others + (filled - at_edge)
-        return edges, others
-
-    edges, others = lax.fori_loop(0, devices, scan, (0, 0), unroll=8)
-    bound_ref[0] = others
+            word = words[q][d]
+            list_ref[word >> 16] = word
+
+    bound_ref[0] = counts[1][0]
 
     def add(word, out):
         band_ref[0] += out[0:128, 0:128]
@@ -245,7 +261,7 @@
         rhs_ref[...] += out[256:264, 0:128]
         spill_ref[128:136, :] += out[256:264, 128:256]
 
-    sweep(edges, lambda i: edge_list[i], recv_ref, add, bufs)
+    sweep(counts[0][0], lambda i: list_ref[i], recv_ref, add, bufs)
 
 
 def inner_kernel(bound_ref, list_ref, recv_ref, edge_band_ref, edge_rhs_ref, band_ref, rhs_ref, *bufs):
@@ -256,14 +272,14 @@
     rhs_ref[last:last + 1] = edge_rhs_ref[0:1, :]
 
     def add(word, out):
-        at = (word >> 8) - 1
+        at = ((word >> 8) & 255) - 1
         band_ref[at, 0] += out[0:128, 0:128]
         band_ref[at, 1] += out[0:128, 128:256]
         band_ref[at + 1, 0] += out[128:256, 128:256]
         rhs_ref[pl.ds(at, 1), :] += out[256:257, 0:128]
         rhs_ref[pl.ds(at + 1, 1), :] += out[256:257, 128:256]
 
-    sweep(bound_ref[0], lambda i: list_ref[i], recv_ref, add, bufs)
+    sweep(bound_ref[0], lambda i: list_ref[recv_ref.shape[0] * CAP - 1 - i], recv_ref, add, bufs)
 
 
 def finish_kernel(band_ref, rhs_ref, spill_ref, band_hbm, rhs_hbm, first_band, first_rhs, sems):
@@ -287,8 +303,8 @@
 def buffers():
     return [
         pltpu.VMEM((2, 8, 128), F32),
-        pltpu.VMEM((2, 192, 128), F32),
-        pltpu.VMEM((2, 272, 128), BF16),
+        pltpu.VMEM((2, 64, 128), F32),
+        pltpu.VMEM((272, 256), BF16),
         pltpu.VMEM((8, 128), F32),
     ] * GROUP
 
@@ -316,8 +332,9 @@
             pltpu.VMEM((8, 128), jnp.int32),
             pltpu.SMEM((128,), jnp.int32),
             pltpu.SMEM((128,), jnp.int32),
-            pltpu.SMEM((devices * CAP + 8,), jnp.int32),
-            pltpu.SemaphoreType.DMA((CAP,)),
+            pltpu.SMEM((128,), jnp.int32),
+            pltpu.SMEM((128,), jnp.int32),
+            pltpu.SemaphoreType.DMA((4,)),
         ]
         + buffers(),
         compiler_params=pltpu.CompilerParams(vmem_limit_bytes=40 * MiB),

time: 86.3 us -> 84.2 us (0.976)
  Pallas kernels: 27.8 us -> 26 us
    pallas_call x1, Pallas kernels: 11.1 us -> 10.2 us  [edge(): pl.pallas_call(edge_kernel, out_shape=(jax.ShapeDtypeStruct((2, 128, 128)...]
  transfers between devices with their start and end apart: 1 -> 1, of which waited for: 0 -> 0; matrix products, arithmetic and copies ran while one was open for 0% -> 0% of each run, Pallas kernels for 12% -> 11%
where the time goes in v5:
time: 84.2 us; the launch traced here: 84 us
  blocking collectives  56.3 us (67%)
  Pallas kernels  26 us (31%)
  starting transfers between devices  1.02 us (1%)
    all_to_all x1, blocking collectives, on_device(): lax.all_to_all(sent, AXES, split_axis=0, concat_axis=0, tiled=True)  56.3 us
    pallas_call x1, Pallas kernels, edge(): pl.pallas_call(edge_kernel, out_shape=(jax.ShapeDtypeStruct((2, 128, 128)...  10.2 us
    pallas_call x1, Pallas kernels, inner(): pl.pallas_call(inner_kernel, out_shape=(jax.ShapeDtypeStruct((BLK_DEV, 2,...  9.48 us
    pallas_call x1, Pallas kernels, pack(): pl.pallas_call(pack_kernel, out_shape=jax.ShapeDtypeStruct((device_count,...  4.78 us
  transfers between devices with their start and end apart: 1, of which 0 were waited for; matrix products, arithmetic and copies ran while one was open for 0% of the time, Pallas kernels for 11%

profile of v5, /device:TPU:1, one launch (start us, length us, event | category | flops | bytes accessed | tf_op | source)
XLA Modules:
  0.0 84.0 jit_solution(1953809295664330805)
XLA Ops:
  0.6 4.8 %pack.1 = bf16[128,13,8,128]{3,2,1,0:T(8,128)(2,1)} custom-call(s32[128]{0:T(128)} %bitcast.2, s32[128]{0:T(128)} %offset_ref.1, s32[1]{0:T(128)} %bitcast.1.me_ref, s32[128,2,4,256]{3,2,1,0:T(4,128)} %index_hbm.1, bf16[128,2,4,256]{3,2,1,0:T(4,128)(2,1)} %frac_hbm.1, bf16[128,2,4,256]{3,2,1,0:T(4,128)(2,1)} %proj_hbm.1, bf16[128,256]{1,0:T(8,128)(2,1)} %force_hbm.1), custom_call_target="tpu_custom_call" | custom-call | tf_op jit(solution)/shard_map/pack/pallas_call | solution.py:80
  5.4 56.3 %all_to_all.5.recv_ref = bf16[128,13,8,128]{3,2,1,0:T(8,128)(2,1)S(1)} all-to-all(bf16[128,13,8,128]{3,2,1,0:T(8,128)(2,1)} %pack.1), channel_id=1, replica_groups=mesh['frame'=4,'panel'=32] {'frame','panel'}, dimensions={0} | all-to-all | bytes 6815744 | tf_op jit(solution)/shard_map/all_to_all | solution.py:382
  61.7 10.2 %edge.1 = (f32[2,128,128]{2,1,0:T(8,128)S(1)}, f32[8,128]{1,0:T(8,128)S(1)}, f32[136,128]{1,0:T(8,128)S(1)}, s32[264]{0:T(512)S(1)}, s32[1]{0:T(128)}) custom-call(bf16[128,13,8,128]{3,2,1,0:T(8,128)(2,1)S(1)} %all_to_all.5.recv_ref), custom_call_target="tpu_custom_call" | custom-call | flops 4294967296 | bytes 4194304 | tf_op jit(solution)/shard_map/edge/pallas_call | solution.py:320
  71.9 1.0 %collective-permute-start = (f32[136,128]{1,0:T(8,128)S(1)}, f32[136,128]{1,0:T(8,128)S(1)}, u32[]{:S(2)}, u32[]{:S(2)}) collective-permute-start(f32[136,128]{1,0:T(8,128)S(1)} %get-tuple-element.15), channel_id=1, source_target_pairs={{0,1},{1,2},{2,3},{3,4},{4,5},{5,6},{6,7},{7,8},{8,9},{9,10},{10,1... | collective-permute-start | bytes 208904 | tf_op jit(solution)/shard_map/ppermute | solution.py:385
  72.9 9.5 %inner.1 = (f32[22,2,128,128]{3,2,1,0:T(8,128)S(1)}, f32[22,128]{1,0:T(8,128)S(1)}) custom-call(s32[1]{0:T(128)} %get-tuple-element.9.bound_ref, s32[264]{0:T(512)S(1)} %get-tuple-element.10.list_ref, bf16[128,13,8,128]{3,2,1,0:T(8,128)(2,1)S(1)} %all_to_all.5.recv_ref, f32[2,128,128]{2,1,0:T(8,128)S(1)} %get-tuple-element.11.edge_band_ref, ...), custom_call_target="tpu_custom_call" | custom-call | flops 4294967296 | bytes 4194304 | tf_op jit(solution)/shard_map/inner/pallas_call | solution.py:347
  82.4 0.0 collective-permute-done.spill_ref
  82.4 1.6 %finish.1 = (f32[22,2,128,128]{3,2,1,0:T(8,128)}, f32[22,128]{1,0:T(8,128)}) custom-call(f32[22,2,128,128]{3,2,1,0:T(8,128)S(1)} %get-tuple-element.13.band_ref, f32[22,128]{1,0:T(8,128)S(1)} %get-tuple-element.14.rhs_ref, f32[136,128]{1,0:T(8,128)S(1)} %collective-permute-done.spill_ref), custom_call_target="tpu_custom_call" | custom-call | tf_op jit(solution)/shard_map/finish/pallas_call | solution.py:363
Async XLA Ops:
  71.9 10.5 %collective-permute-start = (f32[136,128]{1,0:T(8,128)S(1)}, f32[136,128]{1,0:T(8,128)S(1)}, u32[]{:S(2)}, u32[]{:S(2)}) collective-permute-start(f32[136,128]{1,0:T(8,128)S(1)} %get-tuple-element.15), channel_id=1, source_target_pairs={{0,1},{1,2},{2,3},{3,4},{4,5},{5,6},{6,7},{7,8},{8,9},{9,10},{10,1... | collective-permute-start | bytes 208904 | tf_op jit(solution)/shard_map/ppermute | solution.py:385

commit v6 on v5

--- a/solution.py
+++ b/solution.py
@@ -11,15 +11,15 @@
 AXES = ("frame", "panel")
 BF16 = jnp.bfloat16
 F32 = jnp.float32
-CHUNKS = 8
+CHUNKS = 2
 GROUP = 8
 MiB = 1 << 20
 
 
 def pack_kernel(
-    owner_ref, offset_ref, me_ref, index_hbm, frac_hbm, proj_hbm, force_hbm, out_hbm,
-    count_ref, index_ref, frac_ref, proj_ref, force_ref, force_f32, tile_ref, tail_f32, tail_ref,
-    in_sems, force_sem, out_sem, tail_sem,
+    owner_hbm, offset_hbm, index_hbm, frac_hbm, proj_hbm, force_hbm, out_hbm,
+    owner_ref, offset_ref, count_ref, slot_ref, index_ref, frac_ref, proj_ref, force_ref, force_f32, tile_ref, tail_f32, tail_ref,
+    in_sems, force_sem, out_sem, tail_sem, row_sems,
 ):
     device_count = out_hbm.shape[0]
     tiles = owner_ref.shape[0]
@@ -31,7 +31,11 @@
         return pltpu.make_async_copy(arrays[a][0].at[part], arrays[a][1].at[part], in_sems.at[a, c])
 
     force_copy = pltpu.make_async_copy(force_hbm, force_ref, force_sem)
+    owner_copy = pltpu.make_async_copy(owner_hbm, owner_ref, row_sems.at[0])
+    offset_copy = pltpu.make_async_copy(offset_hbm, offset_ref, row_sems.at[1])
     force_copy.start()
+    owner_copy.start()
+    offset_copy.start()
     for c in range(CHUNKS):
         for a in range(3):
             fetch(a, c).start()
@@ -41,49 +45,61 @@
         count_ref[d] = 0
 
     tail_f32[...] = jnp.zeros_like(tail_f32)
-    here = lax.broadcasted_iota(jnp.int32, (1, 128), 1) == me_ref[0]
+    me = lax.axis_index(AXES[0]) * lax.axis_size(AXES[1]) + lax.axis_index(AXES[1])
+    here = lax.broadcasted_iota(jnp.int32, (1, 128), 1) == me
+    owner_copy.wait()
+    offset_copy.wait()
     force_copy.wait()
     force_f32[...] = force_ref[...].astype(F32)
+
+    @pl.loop(0, tiles, unroll=4)
+    def _(t):
+        owner = owner_ref[t]
+        place = count_ref[owner]
+        count_ref[owner] = place + 1
+        slot_ref[t] = owner * CAP + place
+        row = force_f32[pl.ds(t, 1), :]
+        for g in range(2):
+            tail_f32[owner, pl.ds(place * 2 + g, 1), :] = row[:, g * 128 : g * 128 + 128]
+        tail_f32[owner, pl.ds(4 + place, 1), :] = jnp.where(here, (offset_ref[t] + 1).astype(F32), 0.0)
+
+    tail_ref[...] = tail_f32[...].astype(BF16)
+    tail_copy = pltpu.make_async_copy(tail_ref, out_hbm.at[:, 12], tail_sem)
+    tail_copy.start()
 
     for c in range(CHUNKS):
         for a in range(3):
             fetch(a, c).wait()
 
-        @pl.loop(c * step, (c + 1) * step, unroll=2)
+        @pl.loop(c * step, (c + 1) * step, unroll=4)
         def _(t):
-            owner = owner_ref[t]
-            place = count_ref[owner]
-            count_ref[owner] = place + 1
+            slot = slot_ref[t]
             for a in range(3):
                 ref = arrays[a][1]
                 for g in range(2):
                     low = ref[t, 0, :, g * 128 : g * 128 + 128].astype(F32)
                     high = ref[t, 1, :, g * 128 : g * 128 + 128].astype(F32)
                     tile_ref[t, a * 2 + g] = jnp.concatenate([low, high], axis=0).astype(BF16)
-            pltpu.make_async_copy(tile_ref.at[t], out_hbm.at[owner, pl.ds(place * 6, 6)], out_sem).start()
-            row = force_f32[pl.ds(t, 1), :]
-            for g in range(2):
-                tail_f32[owner, pl.ds(place * 2 + g, 1), :] = row[:, g * 128 : g * 128 + 128]
-            tail_f32[owner, pl.ds(4 + place, 1), :] = jnp.where(here, (offset_ref[t] + 1).astype(F32), 0.0)
-
-    tail_ref[...] = tail_f32[...].astype(BF16)
-    tail_copy = pltpu.make_async_copy(tail_ref, out_hbm.at[:, 12], tail_sem)
-    tail_copy.start()
+            target = out_hbm.at[slot >> 1, pl.ds((slot & 1) * 6, 6)]
+            pltpu.make_async_copy(tile_ref.at[t], target, out_sem).start()
+
     tail_copy.wait()
     pltpu.make_async_copy(tile_ref, tile_ref, out_sem).wait()
 
 
-def pack(owners, offsets, me, spline_index, spline_frac, projection, forces, device_count):
+def pack(owners, offsets, spline_index, spline_frac, projection, forces, device_count):
     hbm = pl.BlockSpec(memory_space=pltpu.HBM)
-    smem = pl.BlockSpec(memory_space=pltpu.SMEM)
     tiles = owners.shape[0]
     return pl.pallas_call(
         pack_kernel,
         out_shape=jax.ShapeDtypeStruct((device_count, 13, 8, 128), BF16),
-        in_specs=[smem, smem, smem, hbm, hbm, hbm, hbm],
+        in_specs=[hbm] * 6,
         out_specs=hbm,
         scratch_shapes=[
+            pltpu.SMEM((tiles,), jnp.int32),
+            pltpu.SMEM((tiles,), jnp.int32),
             pltpu.SMEM((device_count,), jnp.int32),
+            pltpu.SMEM((tiles,), jnp.int32),
             pltpu.VMEM(spline_index.shape, spline_index.dtype),
             pltpu.VMEM(spline_frac.shape, BF16),
             pltpu.VMEM(projection.shape, BF16),
@@ -96,10 +112,11 @@
             pltpu.SemaphoreType.DMA,
             pltpu.SemaphoreType.DMA,
             pltpu.SemaphoreType.DMA,
+            pltpu.SemaphoreType.DMA((2,)),
         ],
         compiler_params=pltpu.CompilerParams(vmem_limit_bytes=60 * MiB),
         name="pack",
-    )(owners, offsets, me, spline_index, spline_frac, projection, forces)
+    )(owners, offsets, spline_index, spline_frac, projection, forces)
 
 
 def spline_rows(recv_ref, source, place, scale, bufs):
@@ -210,7 +227,7 @@
 
 
 def edge_kernel(
-    recv_ref, band_ref, rhs_ref, spill_ref, list_ref, bound_ref, meta_i32, first_words, second_words, edge_count,
+    recv_ref, band_ref, rhs_ref, spill_ref, list_ref, meta_i32, first_words, second_words, edge_count,
     other_count, meta_sems, *bufs,
 ):
     counts = (edge_count, other_count)
@@ -252,7 +269,7 @@
             word = words[q][d]
             list_ref[word >> 16] = word
 
-    bound_ref[0] = counts[1][0]
+    list_ref[slots + 1] = counts[1][0]
 
     def add(word, out):
         band_ref[0] += out[0:128, 0:128]
@@ -264,7 +281,10 @@
     sweep(counts[0][0], lambda i: list_ref[i], recv_ref, add, bufs)
 
 
-def inner_kernel(bound_ref, list_ref, recv_ref, edge_band_ref, edge_rhs_ref, band_ref, rhs_ref, *bufs):
+def inner_kernel(list_hbm, recv_ref, edge_band_ref, edge_rhs_ref, band_ref, rhs_ref, list_ref, list_sem, *bufs):
+    list_copy = pltpu.make_async_copy(list_hbm, list_ref, list_sem)
+    list_copy.start()
+    slots = recv_ref.shape[0] * CAP
     last = band_ref.shape[0] - 1
     band_ref[0:last] = jnp.zeros((last, 2, 128, 128), F32)
     band_ref[last] = edge_band_ref[...]
@@ -279,7 +299,8 @@
         rhs_ref[pl.ds(at, 1), :] += out[256:257, 0:128]
         rhs_ref[pl.ds(at + 1, 1), :] += out[256:257, 128:256]
 
-    sweep(bound_ref[0], lambda i: list_ref[recv_ref.shape[0] * CAP - 1 - i], recv_ref, add, bufs)
+    list_copy.wait()
+    sweep(list_ref[slots + 1], lambda i: list_ref[slots - 1 - i], recv_ref, add, bufs)
 
 
 def finish_kernel(band_ref, rhs_ref, spill_ref, band_hbm, rhs_hbm, first_band, first_rhs, sems):
@@ -324,10 +345,9 @@
             jax.ShapeDtypeStruct((8, 128), F32),
             jax.ShapeDtypeStruct((136, 128), F32),
             jax.ShapeDtypeStruct((devices * CAP + 8,), jnp.int32),
-            jax.ShapeDtypeStruct((1,), jnp.int32),
         ),
         in_specs=[VMEM],
-        out_specs=(VMEM, VMEM, VMEM, SMEM, SMEM),
+        out_specs=(VMEM, VMEM, VMEM, SMEM),
         scratch_shapes=[
             pltpu.VMEM((8, 128), jnp.int32),
             pltpu.SMEM((128,), jnp.int32),
@@ -343,20 +363,20 @@
     )(received)
 
 
-def inner(bound, lists, received, edge_band, edge_rhs):
+def inner(lists, received, edge_band, edge_rhs):
     return pl.pallas_call(
         inner_kernel,
         out_shape=(
             jax.ShapeDtypeStruct((BLK_DEV, 2, 128, 128), F32),
             jax.ShapeDtypeStruct((BLK_DEV, 128), F32),
         ),
-        in_specs=[SMEM, SMEM, VMEM, VMEM, VMEM],
+        in_specs=[HBM, VMEM, VMEM, VMEM],
         out_specs=(VMEM, VMEM),
-        scratch_shapes=buffers(),
+        scratch_shapes=[pltpu.SMEM(lists.shape, jnp.int32), pltpu.SemaphoreType.DMA] + buffers(),
         compiler_params=pltpu.CompilerParams(vmem_limit_bytes=40 * MiB),
         cost_estimate=SWEEP_COST,
         name="inner",
-    )(bound, lists, received, edge_band, edge_rhs)
+    )(lists, received, edge_band, edge_rhs)
 
 
 def finish(band, rhs, spill):
@@ -377,13 +397,12 @@
 
 def on_device(spline_index, spline_frac, projection, forces, row_owner, row_offset):
     device_count = lax.axis_size(AXES)
-    me = lax.axis_index(AXES).astype(jnp.int32).reshape(1)
-    sent = pack(row_owner[:, 0], row_offset, me, spline_index, spline_frac, projection, forces, device_count)
+    sent = pack(row_owner[:, 0], row_offset, spline_index, spline_frac, projection, forces, device_count)
     received = lax.all_to_all(sent, AXES, split_axis=0, concat_axis=0, tiled=True)
-    edge_band, edge_rhs, spill, lists, bound = edge(received)
+    edge_band, edge_rhs, spill, lists = edge(received)
     route = [(i, (i + 1) % device_count) for i in range(device_count)]
     spill = lax.ppermute(spill, AXES, route)
-    band, rhs = inner(bound, lists, received, edge_band, edge_rhs)
+    band, rhs = inner(lists, received, edge_band, edge_rhs)
     return finish(band, rhs, spill)
 
 

time: 84.2 us -> 82.3 us (0.977)
  Pallas kernels: 26 us -> 24.2 us
    pallas_call x1, Pallas kernels: 4.78 us -> 3.78 us  [pack(): pl.pallas_call(pack_kernel, out_shape=jax.ShapeDtypeStruct((device_count,...]
where the time goes in v6:
time: 82.3 us; the launch traced here: 82.1 us
  blocking collectives  56.3 us (68%)
  Pallas kernels  24.2 us (29%)
  starting transfers between devices  1 us (1%)
    all_to_all x1, blocking collectives, on_device(): lax.all_to_all(sent, AXES, split_axis=0, concat_axis=0, tiled=True)  56.3 us
    pallas_call x1, Pallas kernels, edge(): pl.pallas_call(edge_kernel, out_shape=(jax.ShapeDtypeStruct((2, 128, 128)...  10.2 us
    pallas_call x1, Pallas kernels, inner(): pl.pallas_call(inner_kernel, out_shape=(jax.ShapeDtypeStruct((BLK_DEV, 2,...  8.65 us
    pallas_call x1, Pallas kernels, pack(): pl.pallas_call(pack_kernel, out_shape=jax.ShapeDtypeStruct((device_count,...  3.78 us
  transfers between devices with their start and end apart: 1, of which 0 were waited for; matrix products, arithmetic and copies ran while one was open for 0% of the time, Pallas kernels for 11%

profile of v6, /device:TPU:1, one launch (start us, length us, event | category | flops | bytes accessed | tf_op | source)
XLA Modules:
  0.0 82.1 jit_solution(3275401116931810025)
XLA Ops:
  0.6 3.8 %pack.1 = bf16[128,13,8,128]{3,2,1,0:T(8,128)(2,1)} custom-call(s32[128]{0:T(128)} %bitcast.1, s32[128]{0:T(128)} %offset_hbm.1, s32[128,2,4,256]{3,2,1,0:T(4,128)} %index_hbm.1, bf16[128,2,4,256]{3,2,1,0:T(4,128)(2,1)} %frac_hbm.1, bf16[128,2,4,256]{3,2,1,0:T(4,128)(2,1)} %proj_hbm.1, bf16[128,256]{1,0:T(8,128)(2,1)} %force_hbm.1), custom_call_target="tpu_custom_call" | custom-call | tf_op jit(solution)/shard_map/pack/pallas_call | solution.py:93
  4.4 56.3 %all_to_all.5.recv_ref = bf16[128,13,8,128]{3,2,1,0:T(8,128)(2,1)S(1)} all-to-all(bf16[128,13,8,128]{3,2,1,0:T(8,128)(2,1)} %pack.1), channel_id=1, replica_groups=mesh['frame'=4,'panel'=32] {'frame','panel'}, dimensions={0} | all-to-all | bytes 6815744 | tf_op jit(solution)/shard_map/all_to_all | solution.py:401
  60.7 10.2 %edge.1 = (f32[2,128,128]{2,1,0:T(8,128)S(1)}, f32[8,128]{1,0:T(8,128)S(1)}, f32[136,128]{1,0:T(8,128)S(1)}, s32[264]{0:T(512)S(1)}) custom-call(bf16[128,13,8,128]{3,2,1,0:T(8,128)(2,1)S(1)} %all_to_all.5.recv_ref), custom_call_target="tpu_custom_call" | custom-call | flops 4294967296 | bytes 4194304 | tf_op jit(solution)/shard_map/edge/pallas_call | solution.py:341
  70.9 1.0 %collective-permute-start = (f32[136,128]{1,0:T(8,128)S(1)}, f32[136,128]{1,0:T(8,128)S(1)}, u32[]{:S(2)}, u32[]{:S(2)}) collective-permute-start(f32[136,128]{1,0:T(8,128)S(1)} %get-tuple-element.13), channel_id=1, source_target_pairs={{0,1},{1,2},{2,3},{3,4},{4,5},{5,6},{6,7},{7,8},{8,9},{9,10},{10,1... | collective-permute-start | bytes 208904 | tf_op jit(solution)/shard_map/ppermute | solution.py:404
  71.9 8.6 %inner.1 = (f32[22,2,128,128]{3,2,1,0:T(8,128)S(1)}, f32[22,128]{1,0:T(8,128)S(1)}) custom-call(s32[264]{0:T(512)S(1)} %get-tuple-element.8.list_hbm, bf16[128,13,8,128]{3,2,1,0:T(8,128)(2,1)S(1)} %all_to_all.5.recv_ref, f32[2,128,128]{2,1,0:T(8,128)S(1)} %get-tuple-element.9.edge_band_ref, f32[8,128]{1,0:T(8,128)S(1)} %get-tuple-element.10.edge_rhs_ref), custom_call_target="tpu_custom_call" | custom-call | flops 4294967296 | bytes 4194304 | tf_op jit(solution)/shard_map/inner/pallas_call | solution.py:367
  80.5 0.0 collective-permute-done.spill_ref
  80.5 1.6 %finish.1 = (f32[22,2,128,128]{3,2,1,0:T(8,128)}, f32[22,128]{1,0:T(8,128)}) custom-call(f32[22,2,128,128]{3,2,1,0:T(8,128)S(1)} %get-tuple-element.11.band_ref, f32[22,128]{1,0:T(8,128)S(1)} %get-tuple-element.12.rhs_ref, f32[136,128]{1,0:T(8,128)S(1)} %collective-permute-done.spill_ref), custom_call_target="tpu_custom_call" | custom-call | tf_op jit(solution)/shard_map/finish/pallas_call | solution.py:383
Async XLA Ops:
  70.9 9.7 %collective-permute-start = (f32[136,128]{1,0:T(8,128)S(1)}, f32[136,128]{1,0:T(8,128)S(1)}, u32[]{:S(2)}, u32[]{:S(2)}) collective-permute-start(f32[136,128]{1,0:T(8,128)S(1)} %get-tuple-element.13), channel_id=1, source_target_pairs={{0,1},{1,2},{2,3},{3,4},{4,5},{5,6},{6,7},{7,8},{8,9},{9,10},{10,1... | collective-permute-start | bytes 208904 | tf_op jit(solution)/shard_map/ppermute | solution.py:404

commit v7 on v6

--- a/solution.py
+++ b/solution.py
@@ -155,7 +155,7 @@
     shift = (k * (1.0 / 8.0) - 7.0 / 16.0).astype(BF16)
     zero = jnp.zeros((16, 128), BF16)
     for s in range(2):
-        blocks = [None] * 16
+        homes, alone, windows = [], [], []
         for n in range(4):
             row = s * 4 + n
             base = [base_buf[g, pl.ds(row, 8, stride=0), :] for g in range(2)]
@@ -163,13 +163,19 @@
             home = (base - shift) + 128
             window = [window_buf[g, row * 8 : row * 8 + 8, :] for g in range(2)]
             window = jnp.concatenate(window, axis=0).astype(BF16)
-            for b in range(16):
-                piece = jnp.where(home == 128 + b, window, zero)
-                blocks[b] = piece if n == 0 else blocks[b] + piece
+            merged = window
+            for p in range(n):
+                merged = merged + jnp.where(homes[p] == home, alone[p], zero)
+            homes.append(home)
+            alone.append(window)
+            windows.append(merged)
         for b in range(16):
+            block = zero
+            for n in range(4):
+                block = jnp.where(homes[n] == 128 + b, windows[n], block)
             at = s * 128 + b * 8
-            design_buf[at : at + 8, 0:128] = blocks[b][0:8]
-            design_buf[at : at + 8, 128:256] = blocks[b][8:16]
+            design_buf[at : at + 8, 0:128] = block[0:8]
+            design_buf[at : at + 8, 128:256] = block[8:16]
 
 
 def force_rows(recv_ref, source, place, bufs):
@@ -194,9 +200,12 @@
 
 def products(bufs):
     design_buf = bufs[2]
-    return lax.dot_general(
-        design_buf[...], design_buf[0:256, :], (((1,), (1,)), ((), ())), preferred_element_type=F32
-    )
+
+    def times(rows, columns):
+        return lax.dot_general(rows, columns, (((1,), (1,)), ((), ())), preferred_element_type=F32)
+
+    rows = jnp.concatenate([design_buf[0:128], design_buf[256:272]], axis=0)
+    return times(rows, design_buf[0:128]), times(design_buf[...], design_buf[128:256])
 
 
 def sweep(count, word_at, recv_ref, add, bufs):
@@ -272,11 +281,12 @@
     list_ref[slots + 1] = counts[1][0]
 
     def add(word, out):
-        band_ref[0] += out[0:128, 0:128]
-        band_ref[1] += out[0:128, 128:256]
-        spill_ref[0:128, :] += out[128:256, 128:256]
-        rhs_ref[...] += out[256:264, 0:128]
-        spill_ref[128:136, :] += out[256:264, 128:256]
+        left, right = out
+        band_ref[0] += left[0:128]
+        band_ref[1] += right[0:128]
+        spill_ref[0:128, :] += right[128:256]
+        rhs_ref[...] += left[128:136]
+        spill_ref[128:136, :] += right[256:264]
 
     sweep(counts[0][0], lambda i: list_ref[i], recv_ref, add, bufs)
 
@@ -293,11 +303,12 @@
 
     def add(word, out):
         at = ((word >> 8) & 255) - 1
-        band_ref[at, 0] += out[0:128, 0:128]
-        band_ref[at, 1] += out[0:128, 128:256]
-        band_ref[at + 1, 0] += out[128:256, 128:256]
-        rhs_ref[pl.ds(at, 1), :] += out[256:257, 0:128]
-        rhs_ref[pl.ds(at + 1, 1), :] += out[256:257, 128:256]
+        left, right = out
+        band_ref[at, 0] += left[0:128]
+        band_ref[at, 1] += right[0:128]
+        band_ref[at + 1, 0] += right[128:256]
+        rhs_ref[pl.ds(at, 1), :] += left[128:129]
+        rhs_ref[pl.ds(at + 1, 1), :] += right[256:257]
 
     list_copy.wait()
     sweep(list_ref[slots + 1], lambda i: list_ref[slots - 1 - i], recv_ref, add, bufs)

time: 82.3 us -> 81.2 us (0.987)
  Pallas kernels: 24.2 us -> 23 us
  transfers between devices with their start and end apart: 1 -> 1, of which waited for: 0 -> 0; matrix products, arithmetic and copies ran while one was open for 0% -> 0% of each run, Pallas kernels for 11% -> 10%
where the time goes in v7:
time: 81.2 us; the launch traced here: 80.9 us
  blocking collectives  56.3 us (69%)
  Pallas kernels  23 us (28%)
  starting transfers between devices  1.02 us (1%)
    all_to_all x1, blocking collectives, on_device(): lax.all_to_all(sent, AXES, split_axis=0, concat_axis=0, tiled=True)  56.3 us
    pallas_call x1, Pallas kernels, edge(): pl.pallas_call(edge_kernel, out_shape=(jax.ShapeDtypeStruct((2, 128, 128)...  9.75 us
    pallas_call x1, Pallas kernels, inner(): pl.pallas_call(inner_kernel, out_shape=(jax.ShapeDtypeStruct((BLK_DEV, 2,...  7.86 us
    pallas_call x1, Pallas kernels, pack(): pl.pallas_call(pack_kernel, out_shape=jax.ShapeDtypeStruct((device_count,...  3.78 us
  transfers between devices with their start and end apart: 1, of which 0 were waited for; matrix products, arithmetic and copies ran while one was open for 0% of the time, Pallas kernels for 10%

profile of v7, /device:TPU:1, one launch (start us, length us, event | category | flops | bytes accessed | tf_op | source)
XLA Modules:
  0.0 80.9 jit_solution(4877925864365404457)
XLA Ops:
  0.6 3.8 %pack.1 = bf16[128,13,8,128]{3,2,1,0:T(8,128)(2,1)} custom-call(s32[128]{0:T(128)} %bitcast.1, s32[128]{0:T(128)} %offset_hbm.1, s32[128,2,4,256]{3,2,1,0:T(4,128)} %index_hbm.1, bf16[128,2,4,256]{3,2,1,0:T(4,128)(2,1)} %frac_hbm.1, bf16[128,2,4,256]{3,2,1,0:T(4,128)(2,1)} %proj_hbm.1, bf16[128,256]{1,0:T(8,128)(2,1)} %force_hbm.1), custom_call_target="tpu_custom_call" | custom-call | tf_op jit(solution)/shard_map/pack/pallas_call | solution.py:93
  4.4 56.3 %all_to_all.5.recv_ref = bf16[128,13,8,128]{3,2,1,0:T(8,128)(2,1)S(1)} all-to-all(bf16[128,13,8,128]{3,2,1,0:T(8,128)(2,1)} %pack.1), channel_id=1, replica_groups=mesh['frame'=4,'panel'=32] {'frame','panel'}, dimensions={0} | all-to-all | bytes 6815744 | tf_op jit(solution)/shard_map/all_to_all | solution.py:412
  60.7 9.8 %edge.1 = (f32[2,128,128]{2,1,0:T(8,128)S(1)}, f32[8,128]{1,0:T(8,128)S(1)}, f32[136,128]{1,0:T(8,128)S(1)}, s32[264]{0:T(512)S(1)}) custom-call(bf16[128,13,8,128]{3,2,1,0:T(8,128)(2,1)S(1)} %all_to_all.5.recv_ref), custom_call_target="tpu_custom_call" | custom-call | flops 4294967296 | bytes 4194304 | tf_op jit(solution)/shard_map/edge/pallas_call | solution.py:352
  70.4 1.0 %collective-permute-start = (f32[136,128]{1,0:T(8,128)S(1)}, f32[136,128]{1,0:T(8,128)S(1)}, u32[]{:S(2)}, u32[]{:S(2)}) collective-permute-start(f32[136,128]{1,0:T(8,128)S(1)} %get-tuple-element.13), channel_id=1, source_target_pairs={{0,1},{1,2},{2,3},{3,4},{4,5},{5,6},{6,7},{7,8},{8,9},{9,10},{10,1... | collective-permute-start | bytes 208904 | tf_op jit(solution)/shard_map/ppermute | solution.py:415
  71.4 7.9 %inner.1 = (f32[22,2,128,128]{3,2,1,0:T(8,128)S(1)}, f32[22,128]{1,0:T(8,128)S(1)}) custom-call(s32[264]{0:T(512)S(1)} %get-tuple-element.8.list_hbm, bf16[128,13,8,128]{3,2,1,0:T(8,128)(2,1)S(1)} %all_to_all.5.recv_ref, f32[2,128,128]{2,1,0:T(8,128)S(1)} %get-tuple-element.9.edge_band_ref, f32[8,128]{1,0:T(8,128)S(1)} %get-tuple-element.10.edge_rhs_ref), custom_call_target="tpu_custom_call" | custom-call | flops 4294967296 | bytes 4194304 | tf_op jit(solution)/shard_map/inner/pallas_call | solution.py:378
  79.3 0.0 collective-permute-done.spill_ref
  79.3 1.6 %finish.1 = (f32[22,2,128,128]{3,2,1,0:T(8,128)}, f32[22,128]{1,0:T(8,128)}) custom-call(f32[22,2,128,128]{3,2,1,0:T(8,128)S(1)} %get-tuple-element.11.band_ref, f32[22,128]{1,0:T(8,128)S(1)} %get-tuple-element.12.rhs_ref, f32[136,128]{1,0:T(8,128)S(1)} %collective-permute-done.spill_ref), custom_call_target="tpu_custom_call" | custom-call | tf_op jit(solution)/shard_map/finish/pallas_call | solution.py:394
Async XLA Ops:
  70.4 8.9 %collective-permute-start = (f32[136,128]{1,0:T(8,128)S(1)}, f32[136,128]{1,0:T(8,128)S(1)}, u32[]{:S(2)}, u32[]{:S(2)}) collective-permute-start(f32[136,128]{1,0:T(8,128)S(1)} %get-tuple-element.13), channel_id=1, source_target_pairs={{0,1},{1,2},{2,3},{3,4},{4,5},{5,6},{6,7},{7,8},{8,9},{9,10},{10,1... | collective-permute-start | bytes 208904 | tf_op jit(solution)/shard_map/ppermute | solution.py:415

commit v8 on v7

--- a/solution.py
+++ b/solution.py
@@ -219,11 +219,11 @@
     def step(j, carry):
         first = j * GROUP
         for u in range(GROUP):
-            out = products(sets[u])
+            add(clamped(first + u - GROUP), products(sets[u]))
+        for u in range(GROUP):
             i = first + u
             scale = jnp.where(i < count, 1.0 / 6.0, 0.0).astype(F32)
             build_tile(recv_ref, clamped(i), scale, sets[u])
-            add(clamped(i - GROUP), out)
         return carry
 
     turns = (count + GROUP - 1) // GROUP

time: 81.2 us -> 81.2 us (level)
  no operation moved by 1% of the time
where the time goes in v8:
time: 81.2 us; the launch traced here: 80.9 us
  blocking collectives  56.3 us (69%)
  Pallas kernels  23 us (28%)
  starting transfers between devices  1.01 us (1%)
    all_to_all x1, blocking collectives, on_device(): lax.all_to_all(sent, AXES, split_axis=0, concat_axis=0, tiled=True)  56.3 us
    pallas_call x1, Pallas kernels, edge(): pl.pallas_call(edge_kernel, out_shape=(jax.ShapeDtypeStruct((2, 128, 128)...  9.75 us
    pallas_call x1, Pallas kernels, inner(): pl.pallas_call(inner_kernel, out_shape=(jax.ShapeDtypeStruct((BLK_DEV, 2,...  7.87 us
    pallas_call x1, Pallas kernels, pack(): pl.pallas_call(pack_kernel, out_shape=jax.ShapeDtypeStruct((device_count,...  3.78 us
  transfers between devices with their start and end apart: 1, of which 0 were waited for; matrix products, arithmetic and copies ran while one was open for 0% of the time, Pallas kernels for 10%

profile of v8, /device:TPU:1, one launch (start us, length us, event | category | flops | bytes accessed | tf_op | source)
XLA Modules:
  0.0 80.9 jit_solution(4877925864365404457)
XLA Ops:
  0.6 3.8 %pack.1 = bf16[128,13,8,128]{3,2,1,0:T(8,128)(2,1)} custom-call(s32[128]{0:T(128)} %bitcast.1, s32[128]{0:T(128)} %offset_hbm.1, s32[128,2,4,256]{3,2,1,0:T(4,128)} %index_hbm.1, bf16[128,2,4,256]{3,2,1,0:T(4,128)(2,1)} %frac_hbm.1, bf16[128,2,4,256]{3,2,1,0:T(4,128)(2,1)} %proj_hbm.1, bf16[128,256]{1,0:T(8,128)(2,1)} %force_hbm.1), custom_call_target="tpu_custom_call" | custom-call | tf_op jit(solution)/shard_map/pack/pallas_call | solution.py:93
  4.4 56.3 %all_to_all.5.recv_ref = bf16[128,13,8,128]{3,2,1,0:T(8,128)(2,1)S(1)} all-to-all(bf16[128,13,8,128]{3,2,1,0:T(8,128)(2,1)} %pack.1), channel_id=1, replica_groups=mesh['frame'=4,'panel'=32] {'frame','panel'}, dimensions={0} | all-to-all | bytes 6815744 | tf_op jit(solution)/shard_map/all_to_all | solution.py:412
  60.7 9.8 %edge.1 = (f32[2,128,128]{2,1,0:T(8,128)S(1)}, f32[8,128]{1,0:T(8,128)S(1)}, f32[136,128]{1,0:T(8,128)S(1)}, s32[264]{0:T(512)S(1)}) custom-call(bf16[128,13,8,128]{3,2,1,0:T(8,128)(2,1)S(1)} %all_to_all.5.recv_ref), custom_call_target="tpu_custom_call" | custom-call | flops 4294967296 | bytes 4194304 | tf_op jit(solution)/shard_map/edge/pallas_call | solution.py:352
  70.4 1.0 %collective-permute-start = (f32[136,128]{1,0:T(8,128)S(1)}, f32[136,128]{1,0:T(8,128)S(1)}, u32[]{:S(2)}, u32[]{:S(2)}) collective-permute-start(f32[136,128]{1,0:T(8,128)S(1)} %get-tuple-element.13), channel_id=1, source_target_pairs={{0,1},{1,2},{2,3},{3,4},{4,5},{5,6},{6,7},{7,8},{8,9},{9,10},{10,1... | collective-permute-start | bytes 208904 | tf_op jit(solution)/shard_map/ppermute | solution.py:415
  71.5 7.9 %inner.1 = (f32[22,2,128,128]{3,2,1,0:T(8,128)S(1)}, f32[22,128]{1,0:T(8,128)S(1)}) custom-call(s32[264]{0:T(512)S(1)} %get-tuple-element.8.list_hbm, bf16[128,13,8,128]{3,2,1,0:T(8,128)(2,1)S(1)} %all_to_all.5.recv_ref, f32[2,128,128]{2,1,0:T(8,128)S(1)} %get-tuple-element.9.edge_band_ref, f32[8,128]{1,0:T(8,128)S(1)} %get-tuple-element.10.edge_rhs_ref), custom_call_target="tpu_custom_call" | custom-call | flops 4294967296 | bytes 4194304 | tf_op jit(solution)/shard_map/inner/pallas_call | solution.py:378
  79.3 0.0 collective-permute-done.spill_ref
  79.3 1.6 %finish.1 = (f32[22,2,128,128]{3,2,1,0:T(8,128)}, f32[22,128]{1,0:T(8,128)}) custom-call(f32[22,2,128,128]{3,2,1,0:T(8,128)S(1)} %get-tuple-element.11.band_ref, f32[22,128]{1,0:T(8,128)S(1)} %get-tuple-element.12.rhs_ref, f32[136,128]{1,0:T(8,128)S(1)} %collective-permute-done.spill_ref), custom_call_target="tpu_custom_call" | custom-call | tf_op jit(solution)/shard_map/finish/pallas_call | solution.py:394
Async XLA Ops:
  70.4 8.9 %collective-permute-start = (f32[136,128]{1,0:T(8,128)S(1)}, f32[136,128]{1,0:T(8,128)S(1)}, u32[]{:S(2)}, u32[]{:S(2)}) collective-permute-start(f32[136,128]{1,0:T(8,128)S(1)} %get-tuple-element.13), channel_id=1, source_target_pairs={{0,1},{1,2},{2,3},{3,4},{4,5},{5,6},{6,7},{7,8},{8,9},{9,10},{10,1... | collective-permute-start | bytes 208904 | tf_op jit(solution)/shard_map/ppermute | solution.py:415
